TPU v7x, 1024 devices: a whole 8x8x8 slice. The times are simulated.
1024 devices in a mesh: gx: 16 (over x_hi, z), gy: 8 (over y), event: 8 (over x_lo, core).
Axes of the slice: x: 8 (x_hi: 2, x_lo: 4; x = x_hi * 4 + x_lo), y: 8, z: 8, core: 2. Of those that a mesh axis runs over, the one named last changes fastest.
Arguments:
- adjoint: float32 [8, 3, 128, 64, 128], P('event', None, 'gx', 'gy'), may hold values from -6 to 6
- velocity: float32 [8, 3, 128, 64, 128], P('event', None, 'gx', 'gy'), may hold values from -2 to 2
- forward: float32 [8, 4, 3, 128, 64, 128], P('event', None, None, 'gx', 'gy'), may hold values from -6 to 6
- receivers: int32 [8, 512], P('event'), may hold values from 0 to 1048575
- residual: float32 [8, 2, 3, 512], P('event'), may hold values from -16 to 16
- params: float32 [3, 32, 16, 32], P(None, 'gx', 'gy'), may hold values from 0.5 to 1.5
Outputs:
- adjoint_end: float32 [8, 3, 128, 64, 128], P('event', None, 'gx', 'gy')
- gradient: float32 [3, 32, 16, 32], P(None, 'gx', 'gy', 'event')
Inputs may be any that keep to these rules, and one draw needn't show every extreme that they name: Flat index (x * 64 + y) * 128 + z of a receiver's cell; several receivers may share a cell.
All inputs are finite; a program needn't handle non-finite values.
Results may differ from a plain program's by a relative error of at most 0.0001.
Values sent between devices are 32-bit elements; how exact they have to be, the bound alone decides.
A program may use at most 32 MiB of HBM per device.

v0:
```python
import math

import jax
import jax.numpy as jnp
from jax import lax
from jax.sharding import PartitionSpec as P

STEP_DT2 = 0.1


def with_halo(block, sides, width):
    for axis, dim in sides:
        count = lax.axis_size(axis)
        forward = [(i, i + 1) for i in range(count - 1)]
        backward = [(target, source) for source, target in forward]
        low = lax.ppermute(
            lax.slice_in_dim(block, block.shape[dim] - width, None, axis=dim), axis, forward
        )
        high = lax.ppermute(lax.slice_in_dim(block, 0, width, axis=dim), axis, backward)
        block = jnp.concatenate([low, block, high], axis=dim)
    return block


def derive_xy(padded):
    inner = padded[:, 1:-1, 1:-1, :]
    zpad = jnp.pad(inner, ((0, 0), (0, 0), (0, 0), (1, 1)))
    along_x = 0.5 * (padded[:, 2:, 1:-1, :] - padded[:, :-2, 1:-1, :])
    along_y = 0.5 * (padded[:, 1:-1, 2:, :] - padded[:, 1:-1, :-2, :])
    along_z = 0.5 * (zpad[:, :, :, 2:] - zpad[:, :, :, :-2])
    return (along_x, along_y, along_z)


def strain_of(along_x, along_y, along_z):
    return jnp.stack(
        [
            along_x[0],
            along_y[1],
            along_z[2],
            0.5 * (along_y[0] + along_x[1]),
            0.5 * (along_z[0] + along_x[2]),
            0.5 * (along_z[1] + along_y[2]),
        ]
    )


def stress_of(strain, lame, shear):
    trace = strain[0] + strain[1] + strain[2]
    normal = lame[None] * trace[None] + 2.0 * shear[None] * strain[:3]
    return jnp.concatenate([normal, 2.0 * shear[None] * strain[3:]], axis=0)


def kernels(strain_adj, strain_fwd, current, accel):
    trace_adj = strain_adj[0] + strain_adj[1] + strain_adj[2]
    trace_fwd = strain_fwd[0] + strain_fwd[1] + strain_fwd[2]
    diag = jnp.sum(strain_adj[:3] * strain_fwd[:3], axis=0)
    offdiag = jnp.sum(strain_adj[3:] * strain_fwd[3:], axis=0)
    return jnp.stack(
        [trace_adj * trace_fwd, 2.0 * diag + 4.0 * offdiag, jnp.sum(current * accel, axis=0)]
    )


def force_local(stress):
    sx, sy, sz = derive_xy(stress)
    return jnp.stack([sx[0] + sy[3] + sz[4], sx[3] + sy[1] + sz[5], sx[4] + sy[5] + sz[2]])


def stress_force(stress):
    padded = with_halo(stress, (("gx", 1), ("gy", 2)), 1)
    return force_local(padded)


def receiver_spots(rec_cells, x_first, y_first, all_y, depth, extent_x, extent_y):
    cell_x = rec_cells // (all_y * depth)
    cell_y = rec_cells // depth % all_y
    cell_z = rec_cells % depth
    local_x = cell_x - x_first
    local_y = cell_y - y_first
    inside = (local_x >= 0) & (local_x < extent_x) & (local_y >= 0) & (local_y < extent_y)
    spots = jnp.where(inside, (local_x * extent_y + local_y) * depth + cell_z, 0)
    return (spots, inside.astype(jnp.float32))


def on_device(adjoint, velocity, forward, receivers, residual, params):
    current = adjoint[0]
    previous = current - velocity[0]
    fwd = forward[0]
    rec_cells = receivers[0]
    res_local = residual[0]
    width_x, width_y, depth = (current.shape[1], current.shape[2], current.shape[3])
    ratio = width_x // params.shape[1]
    steps_all = fwd.shape[0] - 2
    fine = jnp.repeat(jnp.repeat(jnp.repeat(params, ratio, axis=1), ratio, axis=2), ratio, axis=3)
    x_first = lax.axis_index("gx") * width_x
    y_first = lax.axis_index("gy") * width_y
    all_y = width_y * lax.axis_size("gy")
    total = jnp.zeros((3, width_x, width_y, depth), jnp.float32)
    lame, shear, inv_rho = (fine[0], fine[1], 1.0 / fine[2])
    spots, weight = receiver_spots(rec_cells, x_first, y_first, all_y, depth, width_x, width_y)
    for step in range(steps_all):
        both = jnp.concatenate([current, fwd[step + 1]], axis=0)
        padded = with_halo(both, (("gx", 1), ("gy", 2)), 1)
        along_x, along_y, along_z = derive_xy(padded)
        strain_adj = strain_of(along_x[:3], along_y[:3], along_z[:3])
        strain_fwd = strain_of(along_x[3:], along_y[3:], along_z[3:])
        stress = stress_of(strain_adj, lame, shear)
        force = stress_force(stress)
        accel = fwd[step + 2] - 2.0 * fwd[step + 1] + fwd[step]
        total = total + kernels(strain_adj, strain_fwd, current, accel)
        inject = jnp.zeros((3, width_x * width_y * depth), jnp.float32)
        inject = (
            inject.at[:, spots]
            .add(res_local[step] * weight[None])
            .reshape(3, width_x, width_y, depth)
        )
        following = 2.0 * current - previous + STEP_DT2 * inv_rho[None] * (force + inject)
        previous, current = (current, following)
    coarse = total.reshape(
        3, width_x // ratio, ratio, width_y // ratio, ratio, depth // ratio, ratio
    ).sum(axis=(2, 4, 6))
    events_all = adjoint.shape[0] * lax.axis_size("event")
    scale = 1.0 / math.sqrt(ratio**3 * steps_all * events_all)
    summed = lax.psum_scatter(coarse * scale, "event", scatter_dimension=3, tiled=True)
    return (current[None], summed)


def solution(mesh):
    return jax.shard_map(
        on_device,
        mesh=mesh,
        in_specs=(
            P("event", None, "gx", "gy", None),
            P("event", None, "gx", "gy", None),
            P("event", None, None, "gx", "gy", None),
            P("event", None),
            P("event", None, None, None),
            P(None, "gx", "gy", None),
        ),
        out_specs=(P("event", None, "gx", "gy", None), P(None, "gx", "gy", "event")),
        check_vma=False,
    )
```

profile of v0, /device:TPU:72, one launch (start us, length us, event | category | flops | bytes accessed | tf_op | source)
XLA Modules:
  0.0 145.1 jit_solution(3506990379183010042)
XLA Ops:
  0.6 1.0 slice_bitcast_fusion
  1.6 0.7 fusion.71
  2.3 5.2 %collective-permute-start.1 = (f32[6,1,8,128]{3,2,1,0:T(8,128)S(1)}, f32[6,1,8,128]{3,2,1,0:T(8,128)S(1)}, u32[]{:S(2)}, u32[]{:S(2)}) collective-permute-start(f32[6,1,8,128]{3,2,1,0:T(8,128)S(1)} %get-tuple-element.71), channel_id=1, source_target_pairs={{0,64},{64,128},{128,192},{192,256},{256,320},{320,384},{384,448},... | collective-permute-start | bytes 73736 | tf_op jit(solution)/shard_map/ppermute | solution.py:16
  7.5 13.9 %collective-permute-start = (f32[6,1,8,128]{3,2,1,0:T(8,128)S(1)}, f32[6,1,8,128]{3,2,1,0:T(8,128)S(1)}, u32[]{:S(2)}, u32[]{:S(2)}) collective-permute-start(f32[6,1,8,128]{3,2,1,0:T(8,128)S(1)} %get-tuple-element.72), channel_id=1, source_target_pairs={{64,0},{128,64},{192,128},{256,192},{320,256},{384,320},{448,384},... | collective-permute-start | bytes 73736 | tf_op jit(solution)/shard_map/ppermute | solution.py:19
  21.5 0.8 fusion.83
  22.3 0.7 multiply_bitcast_fusion.2
  23.0 1.0 pad_maximum_fusion.71
  24.0 2.2 %collective-permute-start.2 = (f32[6,10,1,128]{3,2,1,0:T(1,128)S(1)}, f32[6,10,1,128]{3,2,1,0:T(1,128)S(1)}, u32[]{:S(2)}, u32[]{:S(2)}) collective-permute-start(f32[6,10,1,128]{3,2,1,0:T(1,128)S(1)} %get-tuple-element.43), channel_id=1, source_target_pairs={{8,0},{16,8},{24,16},{32,24},{40,32},{48,40},{56,48},{9,1},{17,9},... | collective-permute-start | bytes 92168 | tf_op jit(solution)/shard_map/ppermute | solution.py:19
  26.3 3.6 %collective-permute-start.3 = (f32[6,10,1,128]{3,2,1,0:T(1,128)S(1)}, f32[6,10,1,128]{3,2,1,0:T(1,128)S(1)}, u32[]{:S(2)}, u32[]{:S(2)}) collective-permute-start(f32[6,10,1,128]{3,2,1,0:T(1,128)S(1)} %get-tuple-element.44), channel_id=1, source_target_pairs={{0,8},{8,16},{16,24},{24,32},{32,40},{40,48},{48,56},{1,9},{9,17},... | collective-permute-start | bytes 92168 | tf_op jit(solution)/shard_map/ppermute | solution.py:16
  29.9 0.7 and_convert_fusion
  31.4 1.9 %collective-permute-done.3 = f32[6,10,1,128]{3,2,1,0:T(1,128)S(1)} collective-permute-done((f32[6,10,1,128]{3,2,1,0:T(1,128)S(1)}, f32[6,10,1,128]{3,2,1,0:T(1,128)S(1)}, u32[]{:S(2)}, u32[]{:S(2)}) %collective-permute-start.3) | collective-permute-done | bytes 30752 | tf_op jit(solution)/shard_map/ppermute | solution.py:16
  33.3 1.3 fusion.28
  34.9 1.9 %collective-permute-start.5 = (f32[6,1,8,128]{3,2,1,0:T(8,128)S(1)}, f32[6,1,8,128]{3,2,1,0:T(8,128)S(1)}, u32[]{:S(2)}, u32[]{:S(2)}) collective-permute-start(f32[6,1,8,128]{3,2,1,0:T(8,128)S(1)} %get-tuple-element.68), channel_id=1, source_target_pairs={{0,64},{64,128},{128,192},{192,256},{256,320},{320,384},{384,448},... | collective-permute-start | bytes 73736 | tf_op jit(solution)/shard_map/ppermute | solution.py:16
  36.8 10.2 %collective-permute-start.4 = (f32[6,1,8,128]{3,2,1,0:T(8,128)S(1)}, f32[6,1,8,128]{3,2,1,0:T(8,128)S(1)}, u32[]{:S(2)}, u32[]{:S(2)}) collective-permute-start(f32[6,1,8,128]{3,2,1,0:T(8,128)S(1)} %get-tuple-element.69), channel_id=1, source_target_pairs={{64,0},{128,64},{192,128},{256,192},{320,256},{384,320},{448,384},... | collective-permute-start | bytes 73736 | tf_op jit(solution)/shard_map/ppermute | solution.py:19
  47.0 1.5 %collective-permute-done.4 = f32[6,1,8,128]{3,2,1,0:T(8,128)S(1)} collective-permute-done((f32[6,1,8,128]{3,2,1,0:T(8,128)S(1)}, f32[6,1,8,128]{3,2,1,0:T(8,128)S(1)}, u32[]{:S(2)}, u32[]{:S(2)}) %collective-permute-start.4) | collective-permute-done | bytes 24608 | tf_op jit(solution)/shard_map/ppermute | solution.py:19
  48.5 1.9 %collective-permute-start.6 = (f32[6,10,1,128]{3,2,1,0:T(1,128)S(1)}, f32[6,10,1,128]{3,2,1,0:T(1,128)S(1)}, u32[]{:S(2)}, u32[]{:S(2)}) collective-permute-start(f32[6,10,1,128]{3,2,1,0:T(1,128)S(1)} %get-tuple-element.39), channel_id=1, source_target_pairs={{8,0},{16,8},{24,16},{32,24},{40,32},{48,40},{56,48},{9,1},{17,9},... | collective-permute-start | bytes 92168 | tf_op jit(solution)/shard_map/ppermute | solution.py:19
  50.5 3.9 %collective-permute-start.7 = (f32[6,10,1,128]{3,2,1,0:T(1,128)S(1)}, f32[6,10,1,128]{3,2,1,0:T(1,128)S(1)}, u32[]{:S(2)}, u32[]{:S(2)}) collective-permute-start(f32[6,10,1,128]{3,2,1,0:T(1,128)S(1)} %get-tuple-element.40), channel_id=1, source_target_pairs={{0,8},{8,16},{16,24},{24,32},{32,40},{40,48},{48,56},{1,9},{9,17},... | collective-permute-start | bytes 92168 | tf_op jit(solution)/shard_map/ppermute | solution.py:16
  55.0 6.3 %scatter_custom_fusion = f32[3,8192]{0,1:T(8,128)} fusion(s32[512]{0:T(512)S(1)} %bitcast.128, f32[512,3]{1,0:T(8,128)S(1)} %copy.238, f32[]{:T(128)} %constant.71.clone.1), kind=kCustom, calls=%fused_computation.4 | custom fusion | flops 1536 | bytes 98308 | tf_op jit(solution)/shard_map/scatter-add | solution.py:112
  61.3 2.8 %copy.241 = f32[3,8,8,128]{3,2,1,0:T(8,128)S(1)} copy(f32[3,8,8,128]{0,3,2,1:T(8,128)} %bitcast.109) | data formatting | bytes 196608 | tf_op jit(solution)/shard_map/reshape | solution.py:113
  64.6 1.9 %collective-permute-start.9 = (f32[6,1,8,128]{3,2,1,0:T(8,128)S(1)}, f32[6,1,8,128]{3,2,1,0:T(8,128)S(1)}, u32[]{:S(2)}, u32[]{:S(2)}) collective-permute-start(f32[6,1,8,128]{3,2,1,0:T(8,128)S(1)} %get-tuple-element.65), channel_id=1, source_target_pairs={{0,64},{64,128},{128,192},{192,256},{256,320},{320,384},{384,448},... | collective-permute-start | bytes 73736 | tf_op jit(solution)/shard_map/ppermute | solution.py:16
  66.5 10.2 %collective-permute-start.8 = (f32[6,1,8,128]{3,2,1,0:T(8,128)S(1)}, f32[6,1,8,128]{3,2,1,0:T(8,128)S(1)}, u32[]{:S(2)}, u32[]{:S(2)}) collective-permute-start(f32[6,1,8,128]{3,2,1,0:T(8,128)S(1)} %get-tuple-element.66), channel_id=1, source_target_pairs={{64,0},{128,64},{192,128},{256,192},{320,256},{384,320},{448,384},... | collective-permute-start | bytes 73736 | tf_op jit(solution)/shard_map/ppermute | solution.py:19
  76.9 2.9 %copy.239 = f32[1,3,8,8,128]{4,3,2,1,0:T(8,128)S(1)} copy(f32[1,3,8,8,128]{1,4,3,2,0:T(8,128)} %bitcast.110) | data formatting | bytes 196608 | tf_op jit(solution)/shard_map/reshape | solution.py:113
  79.8 6.3 %scatter_custom_fusion.1 = f32[3,8192]{0,1:T(8,128)} fusion(s32[512]{0:T(512)S(1)} %bitcast.129, f32[512,3]{1,0:T(8,128)S(1)} %copy.243, f32[]{:T(128)} %constant.71.clone.1), kind=kCustom, calls=%fused_computation.2 | custom fusion | flops 1536 | bytes 98308 | tf_op jit(solution)/shard_map/scatter-add | solution.py:112
  86.1 2.8 %copy.244 = f32[1,3,8,8,128]{4,3,2,1,0:T(8,128)S(1)} copy(f32[1,3,8,8,128]{1,4,3,2,0:T(8,128)} %bitcast.111) | data formatting | bytes 196608 | tf_op jit(solution)/shard_map/reshape | solution.py:113
  88.9 1.3 dynamic-slice
  90.9 3.1 %collective-permute-start.10 = (f32[6,10,1,128]{3,2,1,0:T(1,128)S(1)}, f32[6,10,1,128]{3,2,1,0:T(1,128)S(1)}, u32[]{:S(2)}, u32[]{:S(2)}) collective-permute-start(f32[6,10,1,128]{3,2,1,0:T(1,128)S(1)} %get-tuple-element.35), channel_id=1, source_target_pairs={{8,0},{16,8},{24,16},{32,24},{40,32},{48,40},{56,48},{9,1},{17,9},... | collective-permute-start | bytes 92168 | tf_op jit(solution)/shard_map/ppermute | solution.py:19
  94.0 2.9 %collective-permute-start.11 = (f32[6,10,1,128]{3,2,1,0:T(1,128)S(1)}, f32[6,10,1,128]{3,2,1,0:T(1,128)S(1)}, u32[]{:S(2)}, u32[]{:S(2)}) collective-permute-start(f32[6,10,1,128]{3,2,1,0:T(1,128)S(1)} %get-tuple-element.36), channel_id=1, source_target_pairs={{0,8},{8,16},{16,24},{24,32},{32,40},{40,48},{48,56},{1,9},{9,17},... | collective-permute-start | bytes 92168 | tf_op jit(solution)/shard_map/ppermute | solution.py:16
  97.0 1.1 add.362
  98.0 0.5 copy.252
  98.5 1.1 stack.91
  99.6 0.5 copy.251
  100.1 1.1 reshape.511
  101.1 0.5 copy.262
  101.6 1.1 reshape.510
  102.7 0.5 copy.253
  103.6 1.9 %collective-permute-start.13 = (f32[6,1,8,128]{3,2,1,0:T(8,128)S(1)}, f32[6,1,8,128]{3,2,1,0:T(8,128)S(1)}, u32[]{:S(2)}, u32[]{:S(2)}) collective-permute-start(f32[6,1,8,128]{3,2,1,0:T(8,128)S(1)} %get-tuple-element.62), channel_id=1, source_target_pairs={{0,64},{64,128},{128,192},{192,256},{256,320},{320,384},{384,448},... | collective-permute-start | bytes 73736 | tf_op jit(solution)/shard_map/ppermute | solution.py:16
  105.5 9.9 %collective-permute-start.12 = (f32[6,1,8,128]{3,2,1,0:T(8,128)S(1)}, f32[6,1,8,128]{3,2,1,0:T(8,128)S(1)}, u32[]{:S(2)}, u32[]{:S(2)}) collective-permute-start(f32[6,1,8,128]{3,2,1,0:T(8,128)S(1)} %get-tuple-element.63), channel_id=1, source_target_pairs={{64,0},{128,64},{192,128},{256,192},{320,256},{384,320},{448,384},... | collective-permute-start | bytes 73736 | tf_op jit(solution)/shard_map/ppermute | solution.py:19
  115.5 1.1 add.370
  116.5 0.5 copy.261
  117.0 1.1 stack.96
  118.1 0.5 copy.260
  118.6 0.2 fusion.4
  118.8 13.9 %all-reduce.4 = f32[3,2,2,32]{3,2,1,0:T(2,128)S(1)} all-reduce(f32[3,2,2,32]{3,2,1,0:T(2,128)S(1)} %broadcast_multiply_fusion), channel_id=2, replica_groups=mesh['gx'=16,'gy'=8,'event'=8] {'event'}, use_global_device_ids=true, to_apply=%region_9.10.clone | all-reduce | flops 384 | bytes 3072
  132.8 4.3 %collective-permute-start.14 = (f32[6,10,1,128]{3,2,1,0:T(1,128)S(1)}, f32[6,10,1,128]{3,2,1,0:T(1,128)S(1)}, u32[]{:S(2)}, u32[]{:S(2)}) collective-permute-start(f32[6,10,1,128]{3,2,1,0:T(1,128)S(1)} %get-tuple-element.31), channel_id=1, source_target_pairs={{8,0},{16,8},{24,16},{32,24},{40,32},{48,40},{56,48},{9,1},{17,9},... | collective-permute-start | bytes 92168 | tf_op jit(solution)/shard_map/ppermute | solution.py:19
  137.1 1.9 %collective-permute-start.15 = (f32[6,10,1,128]{3,2,1,0:T(1,128)S(1)}, f32[6,10,1,128]{3,2,1,0:T(1,128)S(1)}, u32[]{:S(2)}, u32[]{:S(2)}) collective-permute-start(f32[6,10,1,128]{3,2,1,0:T(1,128)S(1)} %get-tuple-element.32), channel_id=1, source_target_pairs={{0,8},{8,16},{16,24},{24,32},{32,40},{40,48},{48,56},{1,9},{9,17},... | collective-permute-start | bytes 92168 | tf_op jit(solution)/shard_map/ppermute | solution.py:16
  139.1 0.7 constant_dynamic-slice_fusion
  139.7 4.4 %collective-permute-done.15 = f32[6,10,1,128]{3,2,1,0:T(1,128)S(1)} collective-permute-done((f32[6,10,1,128]{3,2,1,0:T(1,128)S(1)}, f32[6,10,1,128]{3,2,1,0:T(1,128)S(1)}, u32[]{:S(2)}, u32[]{:S(2)}) %collective-permute-start.15) | collective-permute-done | bytes 30752 | tf_op jit(solution)/shard_map/ppermute | solution.py:16
  144.4 0.7 fusion.33
  (70 shorter events, 2.9 us)
Async XLA Ops:
  0.6 53.8 %copy-start.3 = (s32[1,512]{1,0:T(1,128)S(1)}, s32[1,512]{1,0:T(1,128)}, u32[]{:S(2)}) copy-start(s32[1,512]{1,0:T(1,128)} %param.9) | copy-start | bytes 6148
  2.3 20.7 %collective-permute-start.1 = (f32[6,1,8,128]{3,2,1,0:T(8,128)S(1)}, f32[6,1,8,128]{3,2,1,0:T(8,128)S(1)}, u32[]{:S(2)}, u32[]{:S(2)}) collective-permute-start(f32[6,1,8,128]{3,2,1,0:T(8,128)S(1)} %get-tuple-element.71), channel_id=1, source_target_pairs={{0,64},{64,128},{128,192},{192,256},{256,320},{320,384},{384,448},... | collective-permute-start | bytes 73736 | tf_op jit(solution)/shard_map/ppermute | solution.py:16
  7.5 15.5 %collective-permute-start = (f32[6,1,8,128]{3,2,1,0:T(8,128)S(1)}, f32[6,1,8,128]{3,2,1,0:T(8,128)S(1)}, u32[]{:S(2)}, u32[]{:S(2)}) collective-permute-start(f32[6,1,8,128]{3,2,1,0:T(8,128)S(1)} %get-tuple-element.72), channel_id=1, source_target_pairs={{64,0},{128,64},{192,128},{256,192},{320,256},{384,320},{448,384},... | collective-permute-start | bytes 73736 | tf_op jit(solution)/shard_map/ppermute | solution.py:19
  24.0 7.4 %collective-permute-start.2 = (f32[6,10,1,128]{3,2,1,0:T(1,128)S(1)}, f32[6,10,1,128]{3,2,1,0:T(1,128)S(1)}, u32[]{:S(2)}, u32[]{:S(2)}) collective-permute-start(f32[6,10,1,128]{3,2,1,0:T(1,128)S(1)} %get-tuple-element.43), channel_id=1, source_target_pairs={{8,0},{16,8},{24,16},{32,24},{40,32},{48,40},{56,48},{9,1},{17,9},... | collective-permute-start | bytes 92168 | tf_op jit(solution)/shard_map/ppermute | solution.py:19
  26.3 7.0 %collective-permute-start.3 = (f32[6,10,1,128]{3,2,1,0:T(1,128)S(1)}, f32[6,10,1,128]{3,2,1,0:T(1,128)S(1)}, u32[]{:S(2)}, u32[]{:S(2)}) collective-permute-start(f32[6,10,1,128]{3,2,1,0:T(1,128)S(1)} %get-tuple-element.44), channel_id=1, source_target_pairs={{0,8},{8,16},{16,24},{24,32},{32,40},{40,48},{48,56},{1,9},{9,17},... | collective-permute-start | bytes 92168 | tf_op jit(solution)/shard_map/ppermute | solution.py:16
  34.9 12.2 %collective-permute-start.5 = (f32[6,1,8,128]{3,2,1,0:T(8,128)S(1)}, f32[6,1,8,128]{3,2,1,0:T(8,128)S(1)}, u32[]{:S(2)}, u32[]{:S(2)}) collective-permute-start(f32[6,1,8,128]{3,2,1,0:T(8,128)S(1)} %get-tuple-element.68), channel_id=1, source_target_pairs={{0,64},{64,128},{128,192},{192,256},{256,320},{320,384},{384,448},... | collective-permute-start | bytes 73736 | tf_op jit(solution)/shard_map/ppermute | solution.py:16
  36.8 11.7 %collective-permute-start.4 = (f32[6,1,8,128]{3,2,1,0:T(8,128)S(1)}, f32[6,1,8,128]{3,2,1,0:T(8,128)S(1)}, u32[]{:S(2)}, u32[]{:S(2)}) collective-permute-start(f32[6,1,8,128]{3,2,1,0:T(8,128)S(1)} %get-tuple-element.69), channel_id=1, source_target_pairs={{64,0},{128,64},{192,128},{256,192},{320,256},{384,320},{448,384},... | collective-permute-start | bytes 73736 | tf_op jit(solution)/shard_map/ppermute | solution.py:19
  48.5 15.6 %collective-permute-start.6 = (f32[6,10,1,128]{3,2,1,0:T(1,128)S(1)}, f32[6,10,1,128]{3,2,1,0:T(1,128)S(1)}, u32[]{:S(2)}, u32[]{:S(2)}) collective-permute-start(f32[6,10,1,128]{3,2,1,0:T(1,128)S(1)} %get-tuple-element.39), channel_id=1, source_target_pairs={{8,0},{16,8},{24,16},{32,24},{40,32},{48,40},{56,48},{9,1},{17,9},... | collective-permute-start | bytes 92168 | tf_op jit(solution)/shard_map/ppermute | solution.py:19
  50.5 13.7 %collective-permute-start.7 = (f32[6,10,1,128]{3,2,1,0:T(1,128)S(1)}, f32[6,10,1,128]{3,2,1,0:T(1,128)S(1)}, u32[]{:S(2)}, u32[]{:S(2)}) collective-permute-start(f32[6,10,1,128]{3,2,1,0:T(1,128)S(1)} %get-tuple-element.40), channel_id=1, source_target_pairs={{0,8},{8,16},{16,24},{24,32},{32,40},{40,48},{48,56},{1,9},{9,17},... | collective-permute-start | bytes 92168 | tf_op jit(solution)/shard_map/ppermute | solution.py:16
  55.0 9.5 %copy-start = (f32[1,3,8,8,128]{4,3,2,1,0:T(8,128)S(1)}, f32[1,3,8,8,128]{4,3,2,1,0:T(8,128)}, u32[]{:S(2)}) copy-start(f32[1,3,8,8,128]{4,3,2,1,0:T(8,128)} %param.6) | copy-start | bytes 294916
  55.0 9.5 %copy-start.1 = (f32[1,4,3,8,8,128]{5,4,3,2,1,0:T(8,128)S(1)}, f32[1,4,3,8,8,128]{5,4,3,2,1,0:T(8,128)}, u32[]{:S(2)}) copy-start(f32[1,4,3,8,8,128]{5,4,3,2,1,0:T(8,128)} %param.8) | copy-start | bytes 1179652
  55.0 9.5 %copy-start.2 = (f32[1,3,8,8,128]{4,3,2,1,0:T(8,128)S(1)}, f32[1,3,8,8,128]{4,3,2,1,0:T(8,128)}, u32[]{:S(2)}) copy-start(f32[1,3,8,8,128]{4,3,2,1,0:T(8,128)} %param.7) | copy-start | bytes 294916
  64.6 26.3 %collective-permute-start.9 = (f32[6,1,8,128]{3,2,1,0:T(8,128)S(1)}, f32[6,1,8,128]{3,2,1,0:T(8,128)S(1)}, u32[]{:S(2)}, u32[]{:S(2)}) collective-permute-start(f32[6,1,8,128]{3,2,1,0:T(8,128)S(1)} %get-tuple-element.65), channel_id=1, source_target_pairs={{0,64},{64,128},{128,192},{192,256},{256,320},{320,384},{384,448},... | collective-permute-start | bytes 73736 | tf_op jit(solution)/shard_map/ppermute | solution.py:16
  66.5 24.3 %collective-permute-start.8 = (f32[6,1,8,128]{3,2,1,0:T(8,128)S(1)}, f32[6,1,8,128]{3,2,1,0:T(8,128)S(1)}, u32[]{:S(2)}, u32[]{:S(2)}) collective-permute-start(f32[6,1,8,128]{3,2,1,0:T(8,128)S(1)} %get-tuple-element.66), channel_id=1, source_target_pairs={{64,0},{128,64},{192,128},{256,192},{320,256},{384,320},{448,384},... | collective-permute-start | bytes 73736 | tf_op jit(solution)/shard_map/ppermute | solution.py:19
  90.9 12.2 %collective-permute-start.10 = (f32[6,10,1,128]{3,2,1,0:T(1,128)S(1)}, f32[6,10,1,128]{3,2,1,0:T(1,128)S(1)}, u32[]{:S(2)}, u32[]{:S(2)}) collective-permute-start(f32[6,10,1,128]{3,2,1,0:T(1,128)S(1)} %get-tuple-element.35), channel_id=1, source_target_pairs={{8,0},{16,8},{24,16},{32,24},{40,32},{48,40},{56,48},{9,1},{17,9},... | collective-permute-start | bytes 92168 | tf_op jit(solution)/shard_map/ppermute | solution.py:19
  94.0 9.1 %collective-permute-start.11 = (f32[6,10,1,128]{3,2,1,0:T(1,128)S(1)}, f32[6,10,1,128]{3,2,1,0:T(1,128)S(1)}, u32[]{:S(2)}, u32[]{:S(2)}) collective-permute-start(f32[6,10,1,128]{3,2,1,0:T(1,128)S(1)} %get-tuple-element.36), channel_id=1, source_target_pairs={{0,8},{8,16},{16,24},{24,32},{32,40},{40,48},{48,56},{1,9},{9,17},... | collective-permute-start | bytes 92168 | tf_op jit(solution)/shard_map/ppermute | solution.py:16
  103.6 29.1 %collective-permute-start.13 = (f32[6,1,8,128]{3,2,1,0:T(8,128)S(1)}, f32[6,1,8,128]{3,2,1,0:T(8,128)S(1)}, u32[]{:S(2)}, u32[]{:S(2)}) collective-permute-start(f32[6,1,8,128]{3,2,1,0:T(8,128)S(1)} %get-tuple-element.62), channel_id=1, source_target_pairs={{0,64},{64,128},{128,192},{192,256},{256,320},{320,384},{384,448},... | collective-permute-start | bytes 73736 | tf_op jit(solution)/shard_map/ppermute | solution.py:16
  105.5 27.2 %collective-permute-start.12 = (f32[6,1,8,128]{3,2,1,0:T(8,128)S(1)}, f32[6,1,8,128]{3,2,1,0:T(8,128)S(1)}, u32[]{:S(2)}, u32[]{:S(2)}) collective-permute-start(f32[6,1,8,128]{3,2,1,0:T(8,128)S(1)} %get-tuple-element.63), channel_id=1, source_target_pairs={{64,0},{128,64},{192,128},{256,192},{320,256},{384,320},{448,384},... | collective-permute-start | bytes 73736 | tf_op jit(solution)/shard_map/ppermute | solution.py:19
  132.8 6.9 %collective-permute-start.14 = (f32[6,10,1,128]{3,2,1,0:T(1,128)S(1)}, f32[6,10,1,128]{3,2,1,0:T(1,128)S(1)}, u32[]{:S(2)}, u32[]{:S(2)}) collective-permute-start(f32[6,10,1,128]{3,2,1,0:T(1,128)S(1)} %get-tuple-element.31), channel_id=1, source_target_pairs={{8,0},{16,8},{24,16},{32,24},{40,32},{48,40},{56,48},{9,1},{17,9},... | collective-permute-start | bytes 92168 | tf_op jit(solution)/shard_map/ppermute | solution.py:19
  137.1 7.0 %collective-permute-start.15 = (f32[6,10,1,128]{3,2,1,0:T(1,128)S(1)}, f32[6,10,1,128]{3,2,1,0:T(1,128)S(1)}, u32[]{:S(2)}, u32[]{:S(2)}) collective-permute-start(f32[6,10,1,128]{3,2,1,0:T(1,128)S(1)} %get-tuple-element.32), channel_id=1, source_target_pairs={{0,8},{8,16},{16,24},{24,32},{32,40},{40,48},{48,56},{1,9},{9,17},... | collective-permute-start | bytes 92168 | tf_op jit(solution)/shard_map/ppermute | solution.py:16
where the time goes:
time: 146 us; the launch traced here: 145 us
  starting transfers between devices  79.2 us (54%)
  local copies, waits for them, and re-layouts  22.8 us (16%)
  other arithmetic  19.5 us (13%)
  blocking collectives  13.9 us (10%)
  waiting for transfers between devices  7.78 us (5%)
  between operations  1.93 us (1%)
    ppermute x8, starting transfers between devices, with_halo(): lax.ppermute(lax.slice_in_dim(block, 0, width, axis=dim), axis, backward)  55.9 us
    ppermute x8, starting transfers between devices, with_halo(): lax.ppermute(lax.slice_in_dim(block, block.shape[dim] - width, None, axis...  23.3 us
    unnamed x1, blocking collectives  13.9 us
    scatter-add x2, other arithmetic, on_device(): inject = inject.at[:, spots].add(res_local[step] * weight[None]).reshape(...  12.6 us
    reshape x3, local copies, waits for them, and re-layouts, on_device(): inject = inject.at[:, spots].add(res_local[step] * weight[None]).reshape(...  8.54 us
    ppermute x8, waiting for transfers between devices, with_halo(): lax.ppermute(lax.slice_in_dim(block, block.shape[dim] - width, None, axis...  6.29 us
    another operation x8, local copies, waits for them, and re-layouts, kernels(): jnp.stack([trace_adj * trace_fwd, 2.0 * diag + 4.0 * offdiag, jnp.sum(cur...  6.15 us
    add x4, local copies, waits for them, and re-layouts, kernels(): 2.0 * diag + 4.0 * offdiag  3.05 us
  transfers between devices with their start and end apart: 16, of which 3 were waited for; matrix products, arithmetic and copies ran while one was open for 25% of the time, Pallas kernels for 0%

commit v1 on v0

v1 whole, which is shorter than its diff:
```python
import functools
import math

import jax
import jax.numpy as jnp
from jax import lax
from jax.experimental import pallas as pl
from jax.experimental.pallas import tpu as pltpu
from jax.sharding import PartitionSpec as P

STEP_DT2 = 0.1
MESH = pl.DeviceIdType.MESH
HIGHEST = lax.Precision.HIGHEST
F32 = jnp.float32
BF16 = jnp.bfloat16
B = 8
EXT = 2 * B
DIRS = [(dx, dy) for dx in (-1, 0, 1) for dy in (-1, 0, 1) if (dx, dy) != (0, 0)]
ORDER = sorted(DIRS, key=lambda d: (d[0] == 0, d[0] != 0 and d[1] != 0))


def span(d, w, own):
    if d == 0:
        return pl.ds(0, own), pl.ds(0, own)
    if d < 0:
        return pl.ds(0, w), pl.ds(own, w)
    return pl.ds(own - w, w), pl.ds(2 * own - w, w)


def kernel(sizes, adj, vel, fwd, rec, res, par, aend, grad,
           A, A1, V, F, C, C2, ZF, PF, REC, RES, OH, Q, S, E, PK, T, G,
           lsem, ssem, rsem, gssem, grsem):
    n_gx, n_gy, n_ev, depth, ratio, steps = sizes
    gx, gy, ev = lax.axis_index("gx"), lax.axis_index("gy"), lax.axis_index("event")
    has_x = {-1: gx > 0, 1: gx < n_gx - 1}
    has_y = {-1: gy > 0, 1: gy < n_gy - 1}

    def there(dx, dy):
        if dx == 0:
            return has_y[dy]
        if dy == 0:
            return has_x[dx]
        return jnp.logical_and(has_x[dx], has_y[dy])

    barrier = pltpu.get_barrier_semaphore()
    for dx, dy in ORDER:
        @pl.when(there(dx, dy))
        def _(dx=dx, dy=dy):
            pl.semaphore_signal(barrier, inc=1, device_id={"gx": gx + dx, "gy": gy + dy}, device_id_type=MESH)
    for o in range(1, n_ev):
        pl.semaphore_signal(barrier, inc=1, device_id={"event": lax.rem(ev + o, n_ev)}, device_id_type=MESH)

    own = pl.ds(0, B)
    local = [
        pltpu.make_async_copy(adj.at[0], A.at[:, own, own, :], lsem.at[0]),
        pltpu.make_async_copy(par, C.at[:, pl.ds(0, 2), pl.ds(0, 2), :], lsem.at[1]),
        pltpu.make_async_copy(vel.at[0], V.at[:, own, own, :], lsem.at[2]),
        pltpu.make_async_copy(fwd.at[0], F.at[:, :, own, own, :], lsem.at[3]),
        pltpu.make_async_copy(rec, REC, lsem.at[4]),
        pltpu.make_async_copy(res.at[0], RES, lsem.at[5]),
    ]
    for c in local:
        c.start()

    for d in (-1, 1):
        lo = B + B // 2 if d < 0 else B
        cl = 3 if d < 0 else 2
        x_fill, y_fill = pl.ds(lo, B // 2), pl.ds(lo, B // 2)

        @pl.when(jnp.logical_not(has_x[d]))
        def _(x_fill=x_fill, cl=cl, lo=lo, d=d):
            A[:, x_fill] = jnp.zeros((3, B // 2, EXT, depth), F32)
            V[:, x_fill] = jnp.zeros((3, B // 2, EXT, depth), F32)
            fx = EXT - 1 if d < 0 else B
            for t in range(1, steps + 1):
                F[t, :, fx] = jnp.zeros((3, EXT, depth), F32)
            C[:, cl] = jnp.zeros((3, 4, C.shape[3]), F32)

        @pl.when(jnp.logical_not(has_y[d]))
        def _(y_fill=y_fill, cl=cl):
            A[:, :, y_fill] = jnp.zeros((3, EXT, B // 2, depth), F32)
            V[:, :, y_fill] = jnp.zeros((3, EXT, B // 2, depth), F32)
            for t in range(1, steps + 1):
                F[t, :, :, y_fill] = jnp.zeros((3, EXT, B // 2, depth), F32)
            C[:, :, pl.ds(cl, 1)] = jnp.zeros((3, 4, 1, C.shape[3]), F32)

    count = (1 + has_x[-1].astype(jnp.int32) + has_x[1].astype(jnp.int32)) * (
        1 + has_y[-1].astype(jnp.int32) + has_y[1].astype(jnp.int32)) - 1 + n_ev - 1
    pl.semaphore_wait(barrier, count)

    def message(kind, i, dx, dy):
        corner = dx != 0 and dy != 0
        if kind == 0:
            (sx, tx), (sy, ty) = span(dx, 1, 2), span(dy, 1, 2)
            src, dst = C.at[:, sx, sy, :], C.at[:, tx, ty, :]
        elif kind == 1:
            (sx, tx), (sy, ty) = span(dx, 3 if corner else 4, B), span(dy, 4, B)
            src, dst = A.at[:, sx, sy, :], A.at[:, tx, ty, :]
        elif kind == 2:
            w = 1 if corner else 2
            (sx, tx), (sy, ty) = span(dx, w, B), span(dy, w, B)
            src, dst = V.at[:, sx, sy, :], V.at[:, tx, ty, :]
        else:
            (sx, tx), (sy, ty) = span(dx, 1, B), span(dy, 1, B)
            lv = pl.ds(1, steps)
            src, dst = F.at[lv, :, sx, sy, :], F.at[lv, :, tx, ty, :]
        return pltpu.make_async_remote_copy(
            src_ref=src, dst_ref=dst, send_sem=ssem.at[kind, i], recv_sem=rsem.at[kind, i],
            device_id={"gx": gx + dx, "gy": gy + dy}, device_id_type=MESH)

    def dirs(kind):
        return [(i, d) for i, d in enumerate(ORDER) if kind != 3 or 0 in d]

    def send(kind):
        for i, (dx, dy) in dirs(kind):
            @pl.when(there(dx, dy))
            def _(i=i, dx=dx, dy=dy):
                message(kind, i, dx, dy).start()

    def sent(kind):
        for i, (dx, dy) in dirs(kind):
            @pl.when(there(dx, dy))
            def _(i=i, dx=dx, dy=dy):
                message(kind, i, dx, dy).wait_send()

    def arrived(kind):
        for i, (dx, dy) in dirs(kind):
            @pl.when(there(-dx, -dy))
            def _(i=i, dx=dx, dy=dy):
                message(kind, i, dx, dy).wait_recv()

    local[1].wait()
    send(0)
    local[0].wait()
    send(1)
    local[2].wait()
    send(2)
    local[3].wait()
    send(3)

    local[4].wait()
    local[5].wait()
    cells = REC[...]
    all_y = B * n_gy
    cz = lax.bitwise_and(cells, depth - 1)
    cy = lax.bitwise_and(lax.shift_right_logical(cells, int(math.log2(depth))), all_y - 1)
    cx = lax.shift_right_logical(cells, int(math.log2(depth * all_y)))
    lx, ly = cx - gx * B, cy - gy * B
    half = B // 2
    near = (lx >= -half) & (lx < B + half) & (ly >= -half) & (ly < B + half)
    place = jnp.where(near, lax.bitwise_and(lx, EXT - 1) * EXT + lax.bitwise_and(ly, EXT - 1), -1)
    n_rec = cells.shape[1]
    rows = lax.broadcasted_iota(jnp.int32, (EXT * EXT, n_rec), 0)
    OH[...] = jnp.where(rows == place, 1.0, 0.0).astype(BF16)
    at_z = lax.broadcasted_iota(jnp.int32, (depth, n_rec), 0) == cz

    for n in range(steps):
        for c in range(3):
            left = 2.0 * RES[n, c:c + 1, :]
            spread = jnp.zeros((EXT * EXT, depth), F32)
            for _ in range(3):
                piece = left.astype(BF16).astype(F32)
                left = left - piece
                b = jnp.where(at_z, piece, 0.0).astype(BF16)
                spread = spread + lax.dot_general(OH[...], b, (((1,), (1,)), ((), ())), preferred_element_type=F32)
            Q[3 * n + c] = spread.reshape(EXT, EXT, depth)

    arrived(0)
    nzc = C.shape[3]
    for p in range(3):
        for k in range(4):
            C2[pl.ds(16 * p + 4 * k, 4), :] = C[p, k]
    zi = lax.broadcasted_iota(jnp.int32, (nzc, depth), 0)
    zj = lax.broadcasted_iota(jnp.int32, (nzc, depth), 1)
    widen = jnp.where(zi == zj // ratio, 1.0, 0.0)
    ZF[...] = lax.dot_general(C2[...], widen, (((1,), (0,)), ((), ())), precision=HIGHEST, preferred_element_type=F32)
    row = lax.broadcasted_iota(jnp.int32, (EXT, depth), 0)
    for p in range(3):
        for k in range(4):
            r = [ZF[pl.ds(16 * p + 4 * k + j, 1), :] for j in range(4)]
            fine = jnp.where(row < 4, r[0], jnp.where(row < 8, r[1], jnp.where(row < 12, r[2], r[3])))
            if p == 0:
                PF[0, k] = 0.5 * fine
            elif p == 1:
                PF[1, k] = fine
            else:
                outside = fine == 0.0
                PF[2, k] = jnp.where(outside, 0.0, (0.5 * STEP_DT2) / jnp.where(outside, 1.0, fine))

    lane = lax.broadcasted_iota(jnp.int32, (EXT, depth), 1)
    not_last, not_first = lane < depth - 1, lane > 0

    def along_y(f):
        return pltpu.roll(f, EXT - 1, 0) - pltpu.roll(f, 1, 0)

    def along_z(f):
        return jnp.where(not_last, pltpu.roll(f, depth - 1, 1), 0.0) - jnp.where(not_first, pltpu.roll(f, 1, 1), 0.0)

    def wrap(x):
        return lax.bitwise_and(x, EXT - 1)

    def strain2(field, x):
        up, down = wrap(x + 1), wrap(x - 1)
        mid = [field[c, x] for c in range(3)]
        dx = [field[c, up] - field[c, down] for c in range(3)]
        dy = [along_y(f) for f in mid]
        dz = [along_z(f) for f in mid]
        return dx[0], dy[1], dz[2], dy[0] + dx[1], dz[0] + dx[2], dz[1] + dy[2]

    def stress_loop(field, reach):
        def body(t, carry):
            x = wrap(t + (EXT - reach))
            e = strain2(field, x)
            k = lax.shift_right_logical(x, 2)
            hl, mu = PF[0, k], PF[1, k]
            common = hl * (e[0] + e[1] + e[2])
            hm = 0.5 * mu
            for c in range(3):
                S[c, x] = common + mu * e[c]
                S[3 + c, x] = hm * e[3 + c]
            for c in range(6):
                E[c, x] = e[c][0:B]
            return carry
        lax.fori_loop(0, B + 2 * reach, body, 0)

    def force2(x):
        up, down = wrap(x + 1), wrap(x - 1)
        fx = (S[0, up] - S[0, down]) + along_y(S[3, x]) + along_z(S[4, x])
        fy = (S[3, up] - S[3, down]) + along_y(S[1, x]) + along_z(S[5, x])
        fz = (S[4, up] - S[4, down]) + along_y(S[5, x]) + along_z(S[2, x])
        return fx, fy, fz

    def kernel_sums(field, n):
        def body(k, carry):
            acc = [jnp.zeros((B, depth), F32) for _ in range(3)]
            for j in range(ratio):
                x = ratio * k + j
                f = [v[0:B] for v in strain2(F.at[n + 1], x)]
                e = [E[c, x] for c in range(6)]
                acc[0] = acc[0] + (e[0] + e[1] + e[2]) * (f[0] + f[1] + f[2])
                acc[1] = acc[1] + 2.0 * (e[0] * f[0] + e[1] * f[1] + e[2] * f[2]) + (
                    e[3] * f[3] + e[4] * f[4] + e[5] * f[5])
                for c in range(3):
                    accel = F[n + 2, c, x, 0:B] - 2.0 * F[n + 1, c, x, 0:B] + F[n, c, x, 0:B]
                    acc[2] = acc[2] + field[c, x, 0:B] * accel
            scale = 1.0 / math.sqrt(ratio**3 * steps * n_ev)
            for m, w in enumerate((0.25, 0.25, 1.0)):
                part = acc[m] * (w * scale)
                PK[m, k] = part if n == 0 else PK[m, k] + part
            return carry
        lax.fori_loop(0, B // ratio, body, 0)

    arrived(1)
    stress_loop(A, 3)
    arrived(2)

    def advance(t, carry):
        x = wrap(t + (EXT - 2))
        push = PF[2, lax.shift_right_logical(x, 2)]
        f = force2(x)
        for c in range(3):
            A1[c, x] = A[c, x] + V[c, x] + push * (f[c] + Q[c, x])
        return carry
    lax.fori_loop(0, B + 4, advance, 0)
    arrived(3)
    kernel_sums(A, 0)

    stress_loop(A1, 1)
    kernel_sums(A1, 1)

    kind = 3 * (B // ratio) * B
    ri = lax.broadcasted_iota(jnp.int32, (16, kind), 0)
    ci = lax.broadcasted_iota(jnp.int32, (16, kind), 1)
    pick = jnp.where(ri == ci // ratio, 1.0, 0.0)
    rowsum = lax.dot_general(pick, PK[...].reshape(kind, depth), (((1,), (0,)), ((), ())), precision=HIGHEST,
                             preferred_element_type=F32)
    wide = jnp.concatenate([rowsum[0:8], rowsum[8:16]], axis=1)
    wi = lax.broadcasted_iota(jnp.int32, (2 * depth, depth), 0)
    wj = lax.broadcasted_iota(jnp.int32, (2 * depth, depth), 1)
    narrow = jnp.where(wi // ratio == wj, 1.0, 0.0)
    T[...] = lax.dot_general(wide, narrow, (((1,), (0,)), ((), ())), precision=HIGHEST, preferred_element_type=F32)
    parts = [pltpu.make_async_remote_copy(
        src_ref=T, dst_ref=G.at[o], send_sem=gssem.at[o], recv_sem=grsem.at[o],
        device_id={"event": lax.rem(ev + o, n_ev)}, device_id_type=MESH) for o in range(1, n_ev)]
    for c in parts:
        c.start()

    def finish(x, carry):
        push = PF[2, lax.shift_right_logical(x, 2)]
        f = force2(x)
        for c in range(3):
            new = 2.0 * A1[c, x] - A[c, x] + push * (f[c] + Q[3 + c, x])
            aend[0, c, x] = new[0:B]
        return carry
    lax.fori_loop(0, B, finish, 0)

    total = T[...]
    for o, c in enumerate(parts):
        c.wait_recv()
        total = total + G[o + 1]
    width = nzc // n_ev
    mine = pltpu.roll(total, lax.rem(depth - width * ev, depth), 1)
    other = pltpu.roll(mine, depth - nzc, 1)
    for m in range(3):
        for k in range(2):
            r = 4 * m + 2 * k
            src = mine if r < 8 else other
            grad[m, k] = src[r % 8:r % 8 + 2, 0:width]

    for c in parts:
        c.wait_send()
    for kind_id in range(4):
        sent(kind_id)


def solution(mesh):
    n_gx, n_gy, n_ev = mesh.shape["gx"], mesh.shape["gy"], mesh.shape["event"]

    def on_device(adjoint, velocity, forward, receivers, residual, params):
        depth = adjoint.shape[-1]
        ratio = adjoint.shape[2] // params.shape[1]
        levels = forward.shape[1]
        steps = levels - 2
        nzc = params.shape[3]
        n_rec = receivers.shape[1]
        sizes = (n_gx, n_gy, n_ev, depth, ratio, steps)
        vm = pltpu.VMEM
        return pl.pallas_call(
            functools.partial(kernel, sizes),
            out_shape=(
                jax.ShapeDtypeStruct(adjoint.shape, F32),
                jax.ShapeDtypeStruct((3, params.shape[1], params.shape[2], nzc // n_ev), F32),
            ),
            in_specs=[pl.BlockSpec(memory_space=pl.ANY)] * 6,
            out_specs=(pl.BlockSpec(memory_space=pltpu.VMEM), pl.BlockSpec(memory_space=pltpu.VMEM)),
            scratch_shapes=[
                vm((3, EXT, EXT, depth), F32),
                vm((3, EXT, EXT, depth), F32),
                vm((3, EXT, EXT, depth), F32),
                vm((levels, 3, EXT, EXT, depth), F32),
                vm((3, 4, 4, nzc), F32),
                vm((48, nzc), F32),
                vm((48, depth), F32),
                vm((3, 4, EXT, depth), F32),
                vm((1, n_rec), jnp.int32),
                vm((steps, 3, n_rec), F32),
                vm((EXT * EXT, n_rec), BF16),
                vm((3 * steps, EXT, EXT, depth), F32),
                vm((6, EXT, EXT, depth), F32),
                vm((6, EXT, B, depth), F32),
                vm((3, B // ratio, B, depth), F32),
                vm((8, depth), F32),
                vm((n_ev, 8, depth), F32),
                pltpu.SemaphoreType.DMA((6,)),
                pltpu.SemaphoreType.DMA((4, 8)),
                pltpu.SemaphoreType.DMA((4, 8)),
                pltpu.SemaphoreType.DMA((n_ev,)),
                pltpu.SemaphoreType.DMA((n_ev,)),
            ],
            compiler_params=pltpu.CompilerParams(collective_id=0, has_side_effects=True),
        )(adjoint, velocity, forward, receivers, residual, params)

    return jax.shard_map(
        on_device,
        mesh=mesh,
        in_specs=(
            P("event", None, "gx", "gy", None),
            P("event", None, "gx", "gy", None),
            P("event", None, None, "gx", "gy", None),
            P("event", None),
            P("event", None, None, None),
            P(None, "gx", "gy", None),
        ),
        out_specs=(P("event", None, "gx", "gy", None), P(None, "gx", "gy", "event")),
        check_vma=False,
    )
```

time: 146 us -> 41.5 us (0.28)
  the two profiles are of different devices: /device:TPU:72 before, /device:TPU:63 now
where the time goes in v1:
time: 41.5 us; the launch traced here: 41.2 us
  Pallas kernels  37.1 us (89%)
  local copies, waits for them, and re-layouts  3.46 us (8%)
  between operations  0.65 us (2%)
    pallas_call x1, Pallas kernels, on_device(): pl.pallas_call(functools.partial(kernel, sizes), out_shape=(jax.ShapeDtyp...  37.1 us
    unnamed x5, local copies, waits for them, and re-layouts  3.46 us

profile of v1, /device:TPU:63, one launch (start us, length us, event | category | flops | bytes accessed | tf_op | source)
XLA Modules:
  0.0 41.2 jit_solution(1134814290005766316)
XLA Ops:
  0.6 1.3 %copy.8.res = f32[1,2,3,512]{3,2,1,0:T(4,128)} copy(f32[1,2,3,512]{3,1,2,0:T(2,128)} %param.10) | data formatting | bytes 24576 | tf_op args[4]
  1.9 37.1 %shard_map.77 = (f32[1,3,8,8,128]{4,3,2,1,0:T(8,128)}, f32[3,2,2,4]{3,2,1,0:T(2,128)}) custom-call(f32[1,3,8,8,128]{4,3,2,1,0:T(8,128)} %adj.1, f32[1,3,8,8,128]{4,3,2,1,0:T(8,128)} %vel.1, f32[1,4,3,8,8,128]{5,4,3,2,1,0:T(8,128)} %fwd.1, s32[1,512]{1,0:T(1,128)} %rec.1, f32[1,2,3,512]{3,2,1,0:T(4,128)} %copy.8.res, f32[3,2,2,32]{3,2,1,0:T(2,128)} %par.1), custom_call_target="tpu_custom_call" | custom-call | tf_op jit(solution)/shard_map/pallas_call | solution.py:328
  39.1 0.0 copy-start
  39.1 1.5 %copy.11 = f32[1,3,8,8,128]{4,3,2,1,0:T(8,128)} copy(f32[1,3,8,8,128]{4,3,2,1,0:T(8,128)} %get-tuple-element.4) | data formatting | bytes 196608
  40.6 0.0 copy-done
  40.6 0.6 %copy.12 = f32[3,2,2,4]{3,2,1,0:T(2,128)} copy(f32[3,2,2,4]{3,2,1,0:T(2,128)S(1)} %copy-done) | data formatting | bytes 384
Async XLA Ops:
  39.1 1.6 %copy-start = (f32[3,2,2,4]{3,2,1,0:T(2,128)S(1)}, f32[3,2,2,4]{3,2,1,0:T(2,128)}, u32[]{:S(2)}) copy-start(f32[3,2,2,4]{3,2,1,0:T(2,128)} %get-tuple-element.5) | copy-start | bytes 580

commit v2 on v1

--- a/solution.py
+++ b/solution.py
@@ -28,7 +28,7 @@
 
 
 def kernel(sizes, adj, vel, fwd, rec, res, par, aend, grad,
-           A, A1, V, F, C, C2, ZF, PF, REC, RES, OH, Q, S, E, PK, T, G,
+           A, A1, V, F, C, C2, ZF, PF, REC, RES, OH, Q, S0, S1, E0, E1, FS, AC, KX, T, G,
            lsem, ssem, rsem, gssem, grsem):
     n_gx, n_gy, n_ev, depth, ratio, steps = sizes
     gx, gy, ev = lax.axis_index("gx"), lax.axis_index("gy"), lax.axis_index("event")
@@ -92,18 +92,19 @@
         corner = dx != 0 and dy != 0
         if kind == 0:
             (sx, tx), (sy, ty) = span(dx, 1, 2), span(dy, 1, 2)
-            src, dst = C.at[:, sx, sy, :], C.at[:, tx, ty, :]
+            src, dst = par.at[:, sx, sy, :], C.at[:, tx, ty, :]
         elif kind == 1:
-            (sx, tx), (sy, ty) = span(dx, 3 if corner else 4, B), span(dy, 4, B)
-            src, dst = A.at[:, sx, sy, :], A.at[:, tx, ty, :]
+            w = 3 if corner else 4
+            (sx, tx), (sy, ty) = span(dx, w, B), span(dy, w, B)
+            src, dst = adj.at[0, :, sx, sy, :], A.at[:, tx, ty, :]
         elif kind == 2:
             w = 1 if corner else 2
             (sx, tx), (sy, ty) = span(dx, w, B), span(dy, w, B)
-            src, dst = V.at[:, sx, sy, :], V.at[:, tx, ty, :]
+            src, dst = vel.at[0, :, sx, sy, :], V.at[:, tx, ty, :]
         else:
             (sx, tx), (sy, ty) = span(dx, 1, B), span(dy, 1, B)
             lv = pl.ds(1, steps)
-            src, dst = F.at[lv, :, sx, sy, :], F.at[lv, :, tx, ty, :]
+            src, dst = fwd.at[0, lv, :, sx, sy, :], F.at[lv, :, tx, ty, :]
         return pltpu.make_async_remote_copy(
             src_ref=src, dst_ref=dst, send_sem=ssem.at[kind, i], recv_sem=rsem.at[kind, i],
             device_id={"gx": gx + dx, "gy": gy + dy}, device_id_type=MESH)
@@ -123,20 +124,17 @@
             def _(i=i, dx=dx, dy=dy):
                 message(kind, i, dx, dy).wait_send()
 
-    def arrived(kind):
+    def arrived(kind, from_x):
         for i, (dx, dy) in dirs(kind):
+            if (dx != 0) != from_x:
+                continue
+
             @pl.when(there(-dx, -dy))
             def _(i=i, dx=dx, dy=dy):
                 message(kind, i, dx, dy).wait_recv()
 
-    local[1].wait()
-    send(0)
-    local[0].wait()
-    send(1)
-    local[2].wait()
-    send(2)
-    local[3].wait()
-    send(3)
+    for kind_id in range(4):
+        send(kind_id)
 
     local[4].wait()
     local[5].wait()
@@ -156,7 +154,7 @@
 
     for n in range(steps):
         for c in range(3):
-            left = 2.0 * RES[n, c:c + 1, :]
+            left = 2.0 * RES[c, n:n + 1, :]
             spread = jnp.zeros((EXT * EXT, depth), F32)
             for _ in range(3):
                 piece = left.astype(BF16).astype(F32)
@@ -165,27 +163,30 @@
                 spread = spread + lax.dot_general(OH[...], b, (((1,), (1,)), ((), ())), preferred_element_type=F32)
             Q[3 * n + c] = spread.reshape(EXT, EXT, depth)
 
-    arrived(0)
     nzc = C.shape[3]
-    for p in range(3):
-        for k in range(4):
-            C2[pl.ds(16 * p + 4 * k, 4), :] = C[p, k]
     zi = lax.broadcasted_iota(jnp.int32, (nzc, depth), 0)
     zj = lax.broadcasted_iota(jnp.int32, (nzc, depth), 1)
     widen = jnp.where(zi == zj // ratio, 1.0, 0.0)
-    ZF[...] = lax.dot_general(C2[...], widen, (((1,), (0,)), ((), ())), precision=HIGHEST, preferred_element_type=F32)
     row = lax.broadcasted_iota(jnp.int32, (EXT, depth), 0)
-    for p in range(3):
-        for k in range(4):
-            r = [ZF[pl.ds(16 * p + 4 * k + j, 1), :] for j in range(4)]
-            fine = jnp.where(row < 4, r[0], jnp.where(row < 8, r[1], jnp.where(row < 12, r[2], r[3])))
-            if p == 0:
-                PF[0, k] = 0.5 * fine
-            elif p == 1:
-                PF[1, k] = fine
-            else:
-                outside = fine == 0.0
-                PF[2, k] = jnp.where(outside, 0.0, (0.5 * STEP_DT2) / jnp.where(outside, 1.0, fine))
+
+    def constants(part):
+        for k in range(2 * part, 2 * part + 2):
+            for p in range(3):
+                C2[pl.ds(12 * k + 4 * p, 4), :] = C[p, k]
+        here = pl.ds(24 * part, 24)
+        ZF[here] = lax.dot_general(C2[here], widen, (((1,), (0,)), ((), ())), precision=HIGHEST,
+                                   preferred_element_type=F32)
+        for k in range(2 * part, 2 * part + 2):
+            for p in range(3):
+                r = [ZF[pl.ds(12 * k + 4 * p + j, 1), :] for j in range(4)]
+                fine = jnp.where(row < 4, r[0], jnp.where(row < 8, r[1], jnp.where(row < 12, r[2], r[3])))
+                if p == 0:
+                    PF[0, k] = 0.5 * fine
+                elif p == 1:
+                    PF[1, k] = fine
+                else:
+                    outside = fine == 0.0
+                    PF[2, k] = jnp.where(outside, 0.0, (0.5 * STEP_DT2) / jnp.where(outside, 1.0, fine))
 
     lane = lax.broadcasted_iota(jnp.int32, (EXT, depth), 1)
     not_last, not_first = lane < depth - 1, lane > 0
@@ -198,6 +199,19 @@
 
     def wrap(x):
         return lax.bitwise_and(x, EXT - 1)
+
+    def inner(lo, hi, body):
+        lax.fori_loop(0, hi - lo, lambda t, c: (body(t + lo), c)[1], 0, unroll=2)
+
+    def outer(lo, hi, reach, body):
+        below = lo + reach
+        above = B + reach - hi
+        skip = EXT - B - 2 * reach
+
+        def step(t, carry):
+            body(wrap(t + hi + jnp.where(t >= above, skip, 0)))
+            return carry
+        lax.fori_loop(0, below + above, step, 0, unroll=2)
 
     def strain2(field, x):
         up, down = wrap(x + 1), wrap(x - 1)
@@ -207,9 +221,8 @@
         dz = [along_z(f) for f in mid]
         return dx[0], dy[1], dz[2], dy[0] + dx[1], dz[0] + dx[2], dz[1] + dy[2]
 
-    def stress_loop(field, reach):
-        def body(t, carry):
-            x = wrap(t + (EXT - reach))
+    def stress(field, S, E):
+        def body(x):
             e = strain2(field, x)
             k = lax.shift_right_logical(x, 2)
             hl, mu = PF[0, k], PF[1, k]
@@ -220,59 +233,78 @@
                 S[3 + c, x] = hm * e[3 + c]
             for c in range(6):
                 E[c, x] = e[c][0:B]
-            return carry
-        lax.fori_loop(0, B + 2 * reach, body, 0)
-
-    def force2(x):
+        return body
+
+    def force2(S, x):
         up, down = wrap(x + 1), wrap(x - 1)
         fx = (S[0, up] - S[0, down]) + along_y(S[3, x]) + along_z(S[4, x])
         fy = (S[3, up] - S[3, down]) + along_y(S[1, x]) + along_z(S[5, x])
         fz = (S[4, up] - S[4, down]) + along_y(S[5, x]) + along_z(S[2, x])
         return fx, fy, fz
 
-    def kernel_sums(field, n):
-        def body(k, carry):
-            acc = [jnp.zeros((B, depth), F32) for _ in range(3)]
-            for j in range(ratio):
-                x = ratio * k + j
-                f = [v[0:B] for v in strain2(F.at[n + 1], x)]
-                e = [E[c, x] for c in range(6)]
-                acc[0] = acc[0] + (e[0] + e[1] + e[2]) * (f[0] + f[1] + f[2])
-                acc[1] = acc[1] + 2.0 * (e[0] * f[0] + e[1] * f[1] + e[2] * f[2]) + (
-                    e[3] * f[3] + e[4] * f[4] + e[5] * f[5])
-                for c in range(3):
-                    accel = F[n + 2, c, x, 0:B] - 2.0 * F[n + 1, c, x, 0:B] + F[n, c, x, 0:B]
-                    acc[2] = acc[2] + field[c, x, 0:B] * accel
-            scale = 1.0 / math.sqrt(ratio**3 * steps * n_ev)
-            for m, w in enumerate((0.25, 0.25, 1.0)):
-                part = acc[m] * (w * scale)
-                PK[m, k] = part if n == 0 else PK[m, k] + part
-            return carry
-        lax.fori_loop(0, B // ratio, body, 0)
-
-    arrived(1)
-    stress_loop(A, 3)
-    arrived(2)
-
-    def advance(t, carry):
-        x = wrap(t + (EXT - 2))
+    def advance(x):
         push = PF[2, lax.shift_right_logical(x, 2)]
-        f = force2(x)
+        f = force2(S0, x)
         for c in range(3):
             A1[c, x] = A[c, x] + V[c, x] + push * (f[c] + Q[c, x])
-        return carry
-    lax.fori_loop(0, B + 4, advance, 0)
-    arrived(3)
-    kernel_sums(A, 0)
-
-    stress_loop(A1, 1)
-    kernel_sums(A1, 1)
-
-    kind = 3 * (B // ratio) * B
+
+    def forward_strain(x):
+        for n in range(steps):
+            f = strain2(F.at[n + 1], x)
+            for c in range(6):
+                FS[n, c, x] = f[c][0:B]
+
+    def acceleration(x):
+        for n in range(steps):
+            for c in range(3):
+                AC[n, c, x] = F[n + 2, c, x, 0:B] - 2.0 * F[n + 1, c, x, 0:B] + F[n, c, x, 0:B]
+
+    scale = 1.0 / math.sqrt(ratio**3 * steps * n_ev)
+
+    def kernel_sums(field, E, n):
+        def body(x):
+            e = [E[c, x] for c in range(6)]
+            f = [FS[n, c, x] for c in range(6)]
+            both = (e[0] + e[1] + e[2]) * (f[0] + f[1] + f[2])
+            pure = 2.0 * (e[0] * f[0] + e[1] * f[1] + e[2] * f[2]) + (e[3] * f[3] + e[4] * f[4] + e[5] * f[5])
+            move = field[0, x, 0:B] * AC[n, 0, x] + field[1, x, 0:B] * AC[n, 1, x] + field[2, x, 0:B] * AC[n, 2, x]
+            for m, (v, w) in enumerate(((both, 0.25), (pure, 0.25), (move, 1.0))):
+                v = v * (w * scale)
+                KX[m, x] = v if n == 0 else KX[m, x] + v
+        return body
+
+    for c in local[:4]:
+        c.wait()
+    inner(0, B, acceleration)
+    for kind_id in range(2):
+        arrived(kind_id, False)
+    constants(0)
+    inner(1, B - 1, stress(A, S0, E0))
+    arrived(2, False)
+    inner(2, B - 2, advance)
+    inner(3, B - 3, stress(A1, S1, E1))
+    arrived(3, False)
+    inner(1, B - 1, forward_strain)
+    inner(1, B - 1, kernel_sums(A, E0, 0))
+    inner(3, B - 3, kernel_sums(A1, E1, 1))
+
+    arrived(0, True)
+    constants(1)
+    arrived(1, True)
+    outer(1, B - 1, 3, stress(A, S0, E0))
+    arrived(2, True)
+    outer(2, B - 2, 2, advance)
+    outer(3, B - 3, 1, stress(A1, S1, E1))
+    arrived(3, True)
+    outer(1, B - 1, 0, forward_strain)
+    outer(1, B - 1, 0, kernel_sums(A, E0, 0))
+    outer(3, B - 3, 0, kernel_sums(A1, E1, 1))
+
+    kind = 3 * B * B
     ri = lax.broadcasted_iota(jnp.int32, (16, kind), 0)
     ci = lax.broadcasted_iota(jnp.int32, (16, kind), 1)
-    pick = jnp.where(ri == ci // ratio, 1.0, 0.0)
-    rowsum = lax.dot_general(pick, PK[...].reshape(kind, depth), (((1,), (0,)), ((), ())), precision=HIGHEST,
+    pick = jnp.where(ri == (ci // (ratio * B)) * (B // ratio) + (ci % B) // ratio, 1.0, 0.0)
+    rowsum = lax.dot_general(pick, KX[...].reshape(kind, depth), (((1,), (0,)), ((), ())), precision=HIGHEST,
                              preferred_element_type=F32)
     wide = jnp.concatenate([rowsum[0:8], rowsum[8:16]], axis=1)
     wi = lax.broadcasted_iota(jnp.int32, (2 * depth, depth), 0)
@@ -285,14 +317,13 @@
     for c in parts:
         c.start()
 
-    def finish(x, carry):
+    def finish(x):
         push = PF[2, lax.shift_right_logical(x, 2)]
-        f = force2(x)
+        f = force2(S1, x)
         for c in range(3):
             new = 2.0 * A1[c, x] - A[c, x] + push * (f[c] + Q[3 + c, x])
             aend[0, c, x] = new[0:B]
-        return carry
-    lax.fori_loop(0, B, finish, 0)
+    inner(0, B, finish)
 
     total = T[...]
     for o, c in enumerate(parts):
@@ -328,8 +359,8 @@
         return pl.pallas_call(
             functools.partial(kernel, sizes),
             out_shape=(
-                jax.ShapeDtypeStruct(adjoint.shape, F32),
-                jax.ShapeDtypeStruct((3, params.shape[1], params.shape[2], nzc // n_ev), F32),
+                pltpu.VMEM(adjoint.shape, F32),
+                pltpu.VMEM((3, params.shape[1], params.shape[2], nzc // n_ev), F32),
             ),
             in_specs=[pl.BlockSpec(memory_space=pl.ANY)] * 6,
             out_specs=(pl.BlockSpec(memory_space=pltpu.VMEM), pl.BlockSpec(memory_space=pltpu.VMEM)),
@@ -343,12 +374,16 @@
                 vm((48, depth), F32),
                 vm((3, 4, EXT, depth), F32),
                 vm((1, n_rec), jnp.int32),
-                vm((steps, 3, n_rec), F32),
+                vm((3, steps, n_rec), F32),
                 vm((EXT * EXT, n_rec), BF16),
                 vm((3 * steps, EXT, EXT, depth), F32),
                 vm((6, EXT, EXT, depth), F32),
+                vm((6, EXT, EXT, depth), F32),
                 vm((6, EXT, B, depth), F32),
-                vm((3, B // ratio, B, depth), F32),
+                vm((6, EXT, B, depth), F32),
+                vm((steps, 6, B, B, depth), F32),
+                vm((steps, 3, B, B, depth), F32),
+                vm((3, B, B, depth), F32),
                 vm((8, depth), F32),
                 vm((n_ev, 8, depth), F32),
                 pltpu.SemaphoreType.DMA((6,)),
@@ -358,7 +393,7 @@
                 pltpu.SemaphoreType.DMA((n_ev,)),
             ],
             compiler_params=pltpu.CompilerParams(collective_id=0, has_side_effects=True),
-        )(adjoint, velocity, forward, receivers, residual, params)
+        )(adjoint, velocity, forward, receivers, jnp.swapaxes(residual, 1, 2), params)
 
     return jax.shard_map(
         on_device,

time: 41.5 us -> 36.9 us (0.89)
  local copies, waits for them, and re-layouts: 3.46 us -> 1.24 us
  Pallas kernels: 37.1 us -> 34.9 us
    pallas_call x1, Pallas kernels: 37.1 us -> 34.9 us  [on_device(): pl.pallas_call(functools.partial(kernel, sizes), out_shape=(pltpu.VMEM(ad...]
    unnamed x5 -> x2, local copies, waits for them, and re-layouts: 3.46 us -> 1.24 us
where the time goes in v2:
time: 36.9 us; the launch traced here: 36.7 us
  Pallas kernels  34.9 us (95%)
  local copies, waits for them, and re-layouts  1.24 us (3%)
  between operations  0.64 us (2%)
    pallas_call x1, Pallas kernels, on_device(): pl.pallas_call(functools.partial(kernel, sizes), out_shape=(pltpu.VMEM(ad...  34.9 us
    unnamed x2, local copies, waits for them, and re-layouts  1.24 us

profile of v2, /device:TPU:63, one launch (start us, length us, event | category | flops | bytes accessed | tf_op | source)
XLA Modules:
  0.0 36.7 jit_solution(17663018096192687376)
XLA Ops:
  0.6 34.9 %shard_map.77 = (f32[1,3,8,8,128]{4,3,2,1,0:T(8,128)S(1)}, f32[3,2,2,4]{3,2,1,0:T(2,128)S(1)}) custom-call(f32[1,3,8,8,128]{4,3,2,1,0:T(8,128)} %adj.1, f32[1,3,8,8,128]{4,3,2,1,0:T(8,128)} %vel.1, f32[1,4,3,8,8,128]{5,4,3,2,1,0:T(8,128)} %fwd.1, s32[1,512]{1,0:T(1,128)} %rec.1, f32[1,3,2,512]{3,2,1,0:T(2,128)} %bitcast.1, f32[3,2,2,32]{3,2,1,0:T(2,128)} %par.1), custom_call_target="tpu_custom_call" | custom-call | tf_op jit(solution)/shard_map/pallas_call | solution.py:359
  35.5 0.6 %copy.10 = f32[1,3,8,8,128]{4,3,2,1,0:T(8,128)} copy(f32[1,3,8,8,128]{4,3,2,1,0:T(8,128)S(1)} %get-tuple-element.2) | data formatting | bytes 196608
  36.1 0.6 %copy.11 = f32[3,2,2,4]{3,2,1,0:T(2,128)} copy(f32[3,2,2,4]{3,2,1,0:T(2,128)S(1)} %get-tuple-element.3) | data formatting | bytes 384

commit v3 on v2

--- a/solution.py
+++ b/solution.py
@@ -10,11 +10,11 @@
 
 STEP_DT2 = 0.1
 MESH = pl.DeviceIdType.MESH
-HIGHEST = lax.Precision.HIGHEST
 F32 = jnp.float32
 BF16 = jnp.bfloat16
 B = 8
 EXT = 2 * B
+UNROLL = 4
 DIRS = [(dx, dy) for dx in (-1, 0, 1) for dy in (-1, 0, 1) if (dx, dy) != (0, 0)]
 ORDER = sorted(DIRS, key=lambda d: (d[0] == 0, d[0] != 0 and d[1] != 0))
 
@@ -25,6 +25,18 @@
     if d < 0:
         return pl.ds(0, w), pl.ds(own, w)
     return pl.ds(own - w, w), pl.ds(2 * own - w, w)
+
+
+def times_ones(values, ones):
+    pieces, left = [], values
+    for _ in range(3):
+        piece = left.astype(BF16)
+        pieces.append(piece.astype(F32))
+        left = left - pieces[-1]
+    out = lax.dot_general(jnp.concatenate(pieces, axis=0).astype(BF16), ones.astype(BF16), (((1,), (0,)), ((), ())),
+                          preferred_element_type=F32)
+    n = values.shape[0]
+    return out[0:n] + (out[n:2 * n] + out[2 * n:3 * n])
 
 
 def kernel(sizes, adj, vel, fwd, rec, res, par, aend, grad,
@@ -174,8 +186,7 @@
             for p in range(3):
                 C2[pl.ds(12 * k + 4 * p, 4), :] = C[p, k]
         here = pl.ds(24 * part, 24)
-        ZF[here] = lax.dot_general(C2[here], widen, (((1,), (0,)), ((), ())), precision=HIGHEST,
-                                   preferred_element_type=F32)
+        ZF[here] = times_ones(C2[here], widen)
         for k in range(2 * part, 2 * part + 2):
             for p in range(3):
                 r = [ZF[pl.ds(12 * k + 4 * p + j, 1), :] for j in range(4)]
@@ -188,20 +199,37 @@
                     outside = fine == 0.0
                     PF[2, k] = jnp.where(outside, 0.0, (0.5 * STEP_DT2) / jnp.where(outside, 1.0, fine))
 
-    lane = lax.broadcasted_iota(jnp.int32, (EXT, depth), 1)
+    lane = lax.broadcasted_iota(jnp.int32, (B, depth), 1)
     not_last, not_first = lane < depth - 1, lane > 0
-
-    def along_y(f):
-        return pltpu.roll(f, EXT - 1, 0) - pltpu.roll(f, 1, 0)
-
-    def along_z(f):
-        return jnp.where(not_last, pltpu.roll(f, depth - 1, 1), 0.0) - jnp.where(not_first, pltpu.roll(f, 1, 1), 0.0)
+    sub = lax.broadcasted_iota(jnp.int32, (B, depth), 0)
+    at_top, at_end = sub == 0, sub == B - 1
+
+    def plane(ref, *at, tiles=2):
+        return [ref[(*at, pl.ds(B * t, B))] for t in range(tiles)]
+
+    def along_y(f, tiles=2):
+        out = []
+        for t in range(tiles):
+            a, b = f[t], f[1 - t]
+            out.append(pltpu.roll(jnp.where(at_top, b, a), B - 1, 0) - pltpu.roll(jnp.where(at_end, b, a), 1, 0))
+        return out
+
+    def along_z(f, tiles=2):
+        return [
+            jnp.where(not_last, pltpu.roll(g, depth - 1, 1), 0.0) - jnp.where(not_first, pltpu.roll(g, 1, 1), 0.0)
+            for g in f[:tiles]
+        ]
+
+    def along_x(ref, *at, tiles=2):
+        *at, x = at
+        up, down = plane(ref, *at, wrap(x + 1), tiles=tiles), plane(ref, *at, wrap(x - 1), tiles=tiles)
+        return [a - b for a, b in zip(up, down)]
 
     def wrap(x):
         return lax.bitwise_and(x, EXT - 1)
 
     def inner(lo, hi, body):
-        lax.fori_loop(0, hi - lo, lambda t, c: (body(t + lo), c)[1], 0, unroll=2)
+        lax.fori_loop(0, hi - lo, lambda t, c: (body(t + lo), c)[1], 0, unroll=UNROLL)
 
     def outer(lo, hi, reach, body):
         below = lo + reach
@@ -211,48 +239,52 @@
         def step(t, carry):
             body(wrap(t + hi + jnp.where(t >= above, skip, 0)))
             return carry
-        lax.fori_loop(0, below + above, step, 0, unroll=2)
-
-    def strain2(field, x):
-        up, down = wrap(x + 1), wrap(x - 1)
-        mid = [field[c, x] for c in range(3)]
-        dx = [field[c, up] - field[c, down] for c in range(3)]
-        dy = [along_y(f) for f in mid]
-        dz = [along_z(f) for f in mid]
-        return dx[0], dy[1], dz[2], dy[0] + dx[1], dz[0] + dx[2], dz[1] + dy[2]
+        lax.fori_loop(0, below + above, step, 0, unroll=True)
+
+    def strain2(field, x, tiles=2):
+        mid = [plane(field, c, x) for c in range(3)]
+        dx = [along_x(field, c, x, tiles=tiles) for c in range(3)]
+        dy = [along_y(f, tiles) for f in mid]
+        dz = [along_z(f, tiles) for f in mid]
+        return [
+            (dx[0][t], dy[1][t], dz[2][t], dy[0][t] + dx[1][t], dz[0][t] + dx[2][t], dz[1][t] + dy[2][t])
+            for t in range(tiles)
+        ]
 
     def stress(field, S, E):
         def body(x):
-            e = strain2(field, x)
+            strains = strain2(field, x)
             k = lax.shift_right_logical(x, 2)
-            hl, mu = PF[0, k], PF[1, k]
-            common = hl * (e[0] + e[1] + e[2])
-            hm = 0.5 * mu
+            for t, e in enumerate(strains):
+                rows_t = pl.ds(B * t, B)
+                hl, mu = PF[0, k, rows_t], PF[1, k, rows_t]
+                common = hl * (e[0] + e[1] + e[2])
+                hm = 0.5 * mu
+                for c in range(3):
+                    S[c, x, rows_t] = common + mu * e[c]
+                    S[3 + c, x, rows_t] = hm * e[3 + c]
+            for c in range(6):
+                E[c, x] = strains[0][c]
+        return body
+
+    def force2(S, x, tiles=2):
+        y = [along_y(plane(S, c, x), tiles) for c in (3, 1, 5)]
+        z = [along_z(plane(S, c, x), tiles) for c in (4, 5, 2)]
+        d = [along_x(S, c, x, tiles=tiles) for c in (0, 3, 4)]
+        return [[d[c][t] + y[c][t] + z[c][t] for c in range(3)] for t in range(tiles)]
+
+    def advance(x):
+        for t, f in enumerate(force2(S0, x)):
+            rows_t = pl.ds(B * t, B)
+            push = PF[2, lax.shift_right_logical(x, 2), rows_t]
             for c in range(3):
-                S[c, x] = common + mu * e[c]
-                S[3 + c, x] = hm * e[3 + c]
-            for c in range(6):
-                E[c, x] = e[c][0:B]
-        return body
-
-    def force2(S, x):
-        up, down = wrap(x + 1), wrap(x - 1)
-        fx = (S[0, up] - S[0, down]) + along_y(S[3, x]) + along_z(S[4, x])
-        fy = (S[3, up] - S[3, down]) + along_y(S[1, x]) + along_z(S[5, x])
-        fz = (S[4, up] - S[4, down]) + along_y(S[5, x]) + along_z(S[2, x])
-        return fx, fy, fz
-
-    def advance(x):
-        push = PF[2, lax.shift_right_logical(x, 2)]
-        f = force2(S0, x)
-        for c in range(3):
-            A1[c, x] = A[c, x] + V[c, x] + push * (f[c] + Q[c, x])
+                A1[c, x, rows_t] = A[c, x, rows_t] + V[c, x, rows_t] + push * (f[c] + Q[c, x, rows_t])
 
     def forward_strain(x):
         for n in range(steps):
-            f = strain2(F.at[n + 1], x)
+            (f,) = strain2(F.at[n + 1], x, 1)
             for c in range(6):
-                FS[n, c, x] = f[c][0:B]
+                FS[n, c, x] = f[c]
 
     def acceleration(x):
         for n in range(steps):
@@ -300,17 +332,23 @@
     outer(1, B - 1, 0, kernel_sums(A, E0, 0))
     outer(3, B - 3, 0, kernel_sums(A1, E1, 1))
 
-    kind = 3 * B * B
-    ri = lax.broadcasted_iota(jnp.int32, (16, kind), 0)
-    ci = lax.broadcasted_iota(jnp.int32, (16, kind), 1)
-    pick = jnp.where(ri == (ci // (ratio * B)) * (B // ratio) + (ci % B) // ratio, 1.0, 0.0)
-    rowsum = lax.dot_general(pick, KX[...].reshape(kind, depth), (((1,), (0,)), ((), ())), precision=HIGHEST,
-                             preferred_element_type=F32)
-    wide = jnp.concatenate([rowsum[0:8], rowsum[8:16]], axis=1)
+    sums = []
+    for m in range(3):
+        for k in range(B // ratio):
+            v = sum(KX[m, ratio * k + j] for j in range(1, ratio)) + KX[m, ratio * k]
+            v = v + pltpu.roll(v, B - 1, 0)
+            sums.append(v + pltpu.roll(v, B - 2, 0))
+    spot = lax.bitwise_and(sub, 3)
+    halves = []
+    for at in (0, 4):
+        v = sums[at]
+        for j in range(1, min(4, len(sums) - at)):
+            v = jnp.where(spot == j, pltpu.roll(sums[at + j], j, 0), v)
+        halves.append(v)
+    wide = jnp.concatenate(halves, axis=1)
     wi = lax.broadcasted_iota(jnp.int32, (2 * depth, depth), 0)
     wj = lax.broadcasted_iota(jnp.int32, (2 * depth, depth), 1)
-    narrow = jnp.where(wi // ratio == wj, 1.0, 0.0)
-    T[...] = lax.dot_general(wide, narrow, (((1,), (0,)), ((), ())), precision=HIGHEST, preferred_element_type=F32)
+    T[...] = times_ones(wide, jnp.where(wi // ratio == wj, 1.0, 0.0))
     parts = [pltpu.make_async_remote_copy(
         src_ref=T, dst_ref=G.at[o], send_sem=gssem.at[o], recv_sem=grsem.at[o],
         device_id={"event": lax.rem(ev + o, n_ev)}, device_id_type=MESH) for o in range(1, n_ev)]
@@ -318,12 +356,15 @@
         c.start()
 
     def finish(x):
-        push = PF[2, lax.shift_right_logical(x, 2)]
-        f = force2(S1, x)
+        (f,) = force2(S1, x, 1)
+        push = PF[2, lax.shift_right_logical(x, 2), 0:B]
         for c in range(3):
-            new = 2.0 * A1[c, x] - A[c, x] + push * (f[c] + Q[3 + c, x])
-            aend[0, c, x] = new[0:B]
+            aend[0, c, x] = 2.0 * A1[c, x, 0:B] - A[c, x, 0:B] + push * (f[c] + Q[3 + c, x, 0:B])
     inner(0, B, finish)
+    for kind_id in range(4):
+        sent(kind_id)
+    for c in parts:
+        c.wait_send()
 
     total = T[...]
     for o, c in enumerate(parts):
@@ -334,14 +375,18 @@
     other = pltpu.roll(mine, depth - nzc, 1)
     for m in range(3):
         for k in range(2):
-            r = 4 * m + 2 * k
-            src = mine if r < 8 else other
-            grad[m, k] = src[r % 8:r % 8 + 2, 0:width]
-
-    for c in parts:
-        c.wait_send()
-    for kind_id in range(4):
-        sent(kind_id)
+            i = 2 * m + k
+            src = mine if i < 4 else other
+            for y in range(2):
+                grad[m, k, y:y + 1] = src[4 * y + i % 4:4 * y + i % 4 + 1, 0:width]
+
+
+def put_out(aend, grad, aend_out, grad_out, sems):
+    copies = [pltpu.make_async_copy(aend, aend_out, sems.at[0]), pltpu.make_async_copy(grad, grad_out, sems.at[1])]
+    for c in copies:
+        c.start()
+    for c in copies:
+        c.wait()
 
 
 def solution(mesh):
@@ -356,7 +401,7 @@
         n_rec = receivers.shape[1]
         sizes = (n_gx, n_gy, n_ev, depth, ratio, steps)
         vm = pltpu.VMEM
-        return pl.pallas_call(
+        held = pl.pallas_call(
             functools.partial(kernel, sizes),
             out_shape=(
                 pltpu.VMEM(adjoint.shape, F32),
@@ -394,6 +439,13 @@
             ],
             compiler_params=pltpu.CompilerParams(collective_id=0, has_side_effects=True),
         )(adjoint, velocity, forward, receivers, jnp.swapaxes(residual, 1, 2), params)
+        return pl.pallas_call(
+            put_out,
+            out_shape=tuple(jax.ShapeDtypeStruct(h.shape, F32) for h in held),
+            in_specs=[pl.BlockSpec(memory_space=pltpu.VMEM)] * 2,
+            out_specs=(pl.BlockSpec(memory_space=pl.ANY),) * 2,
+            scratch_shapes=[pltpu.SemaphoreType.DMA((2,))],
+        )(*[pltpu.with_memory_space_constraint(h, pltpu.VMEM) for h in held])
 
     return jax.shard_map(
         on_device,

time: 36.9 us -> 35.5 us (0.962)
  local copies, waits for them, and re-layouts: 1.24 us -> 0 us
    unnamed x2 -> x0, local copies, waits for them, and re-layouts: 1.24 us -> none
    pallas_call x1, Pallas kernels: 34.9 us -> 34 us  [on_device(): pl.pallas_call(functools.partial(kernel, sizes), out_shape=(pltpu.VMEM(ad...]
    pallas_call x0 -> x1, Pallas kernels: none -> 0.66 us  [on_device(): pl.pallas_call(put_out, out_shape=tuple((jax.ShapeDtypeStruct(h.shape, F3...]
where the time goes in v3:
time: 35.5 us; the launch traced here: 35.3 us
  Pallas kernels  34.7 us (98%)
  between operations  0.64 us (2%)
    pallas_call x1, Pallas kernels, on_device(): pl.pallas_call(functools.partial(kernel, sizes), out_shape=(pltpu.VMEM(ad...  34 us

profile of v3, /device:TPU:63, one launch (start us, length us, event | category | flops | bytes accessed | tf_op | source)
XLA Modules:
  0.0 35.3 jit_solution(11588164127445941253)
XLA Ops:
  0.6 34.0 %shard_map.77 = (f32[1,3,8,8,128]{4,3,2,1,0:T(8,128)S(1)}, f32[3,2,2,4]{3,2,1,0:T(2,128)S(1)}) custom-call(f32[1,3,8,8,128]{4,3,2,1,0:T(8,128)} %adj.1, f32[1,3,8,8,128]{4,3,2,1,0:T(8,128)} %vel.1, f32[1,4,3,8,8,128]{5,4,3,2,1,0:T(8,128)} %fwd.1, s32[1,512]{1,0:T(1,128)} %rec.1, f32[1,3,2,512]{3,2,1,0:T(2,128)} %bitcast.1, f32[3,2,2,32]{3,2,1,0:T(2,128)} %par.1), custom_call_target="tpu_custom_call" | custom-call | tf_op jit(solution)/shard_map/pallas_call | solution.py:404
  34.7 0.7 %shard_map.78 = (f32[1,3,8,8,128]{4,3,2,1,0:T(8,128)}, f32[3,2,2,4]{3,2,1,0:T(2,128)}) custom-call(f32[1,3,8,8,128]{4,3,2,1,0:T(8,128)S(1)} %get-tuple-element.4.aend, f32[3,2,2,4]{3,2,1,0:T(2,128)S(1)} %get-tuple-element.5.grad), custom_call_target="tpu_custom_call" | custom-call | tf_op jit(solution)/shard_map/pallas_call | solution.py:442

commit v4 on v3

--- a/solution.py
+++ b/solution.py
@@ -41,7 +41,7 @@
 
 def kernel(sizes, adj, vel, fwd, rec, res, par, aend, grad,
            A, A1, V, F, C, C2, ZF, PF, REC, RES, OH, Q, S0, S1, E0, E1, FS, AC, KX, T, G,
-           lsem, ssem, rsem, gssem, grsem):
+           lsem, ssem, rsem, gssem, grsem, gate):
     n_gx, n_gy, n_ev, depth, ratio, steps = sizes
     gx, gy, ev = lax.axis_index("gx"), lax.axis_index("gy"), lax.axis_index("event")
     has_x = {-1: gx > 0, 1: gx < n_gx - 1}
@@ -54,13 +54,43 @@
             return has_x[dx]
         return jnp.logical_and(has_x[dx], has_y[dy])
 
+    n_z, n_x = n_gx // 2, n_ev
+
+    def turn(px, py, pe):
+        z, y = lax.rem(px, n_z), py
+        x, core = (px // n_z) * (n_ev // 2) + pe // 2, lax.rem(pe, 2)
+
+        def hops(v, n):
+            return v + (2 * v > n).astype(jnp.int32) * (n - 2 * v)
+        place = ((z * n_gy + y) * n_x + x) * 2 + core
+        root = (place == 0).astype(jnp.int32)
+        late = 13 * place - 400 * core + 800 * (hops(z, n_z) + hops(y, n_gy) + hops(x, n_x)) + root * 20000
+        return late * 2048 + place
+
+    my_turn = turn(gx, gy, ev)
+    mates = []
+    for dx, dy in ORDER:
+        exists = there(dx, dy)
+        mates.append((exists, turn(gx + dx, gy + dy, ev) > my_turn, {"gx": gx + dx, "gy": gy + dy}))
+    for o in range(1, n_ev):
+        mate = lax.rem(ev + o, n_ev)
+        mates.append((None, turn(gx, gy, mate) > my_turn, {"event": mate}))
+    later, earlier = [], []
+    for exists, after, _ in mates:
+        later.append(after if exists is None else jnp.logical_and(exists, after))
+        before = jnp.logical_not(after)
+        earlier.append(before if exists is None else jnp.logical_and(exists, before))
+
     barrier = pltpu.get_barrier_semaphore()
-    for dx, dy in ORDER:
-        @pl.when(there(dx, dy))
-        def _(dx=dx, dy=dy):
-            pl.semaphore_signal(barrier, inc=1, device_id={"gx": gx + dx, "gy": gy + dy}, device_id_type=MESH)
-    for o in range(1, n_ev):
-        pl.semaphore_signal(barrier, inc=1, device_id={"event": lax.rem(ev + o, n_ev)}, device_id_type=MESH)
+    for (_, _, device), cond in zip(mates, later):
+        @pl.when(cond)
+        def _(device=device):
+            pl.semaphore_signal(barrier, inc=1, device_id=device, device_id_type=MESH)
+    greetings = sum(c.astype(jnp.int32) for c in earlier)
+
+    @pl.when(greetings > 0)
+    def _():
+        pl.semaphore_wait(barrier, greetings)
 
     own = pl.ds(0, B)
     local = [
@@ -71,35 +101,6 @@
         pltpu.make_async_copy(rec, REC, lsem.at[4]),
         pltpu.make_async_copy(res.at[0], RES, lsem.at[5]),
     ]
-    for c in local:
-        c.start()
-
-    for d in (-1, 1):
-        lo = B + B // 2 if d < 0 else B
-        cl = 3 if d < 0 else 2
-        x_fill, y_fill = pl.ds(lo, B // 2), pl.ds(lo, B // 2)
-
-        @pl.when(jnp.logical_not(has_x[d]))
-        def _(x_fill=x_fill, cl=cl, lo=lo, d=d):
-            A[:, x_fill] = jnp.zeros((3, B // 2, EXT, depth), F32)
-            V[:, x_fill] = jnp.zeros((3, B // 2, EXT, depth), F32)
-            fx = EXT - 1 if d < 0 else B
-            for t in range(1, steps + 1):
-                F[t, :, fx] = jnp.zeros((3, EXT, depth), F32)
-            C[:, cl] = jnp.zeros((3, 4, C.shape[3]), F32)
-
-        @pl.when(jnp.logical_not(has_y[d]))
-        def _(y_fill=y_fill, cl=cl):
-            A[:, :, y_fill] = jnp.zeros((3, EXT, B // 2, depth), F32)
-            V[:, :, y_fill] = jnp.zeros((3, EXT, B // 2, depth), F32)
-            for t in range(1, steps + 1):
-                F[t, :, :, y_fill] = jnp.zeros((3, EXT, B // 2, depth), F32)
-            C[:, :, pl.ds(cl, 1)] = jnp.zeros((3, 4, 1, C.shape[3]), F32)
-
-    count = (1 + has_x[-1].astype(jnp.int32) + has_x[1].astype(jnp.int32)) * (
-        1 + has_y[-1].astype(jnp.int32) + has_y[1].astype(jnp.int32)) - 1 + n_ev - 1
-    pl.semaphore_wait(barrier, count)
-
     def message(kind, i, dx, dy):
         corner = dx != 0 and dy != 0
         if kind == 0:
@@ -124,11 +125,24 @@
     def dirs(kind):
         return [(i, d) for i, d in enumerate(ORDER) if kind != 3 or 0 in d]
 
-    def send(kind):
-        for i, (dx, dy) in dirs(kind):
-            @pl.when(there(dx, dy))
-            def _(i=i, dx=dx, dy=dy):
+    def send(kind, i, cond):
+        dx, dy = ORDER[i]
+        if kind != 3 or 0 in (dx, dy):
+            @pl.when(cond)
+            def _():
                 message(kind, i, dx, dy).start()
+
+    def answered(i, cond):
+        @pl.when(cond)
+        def _():
+            pl.semaphore_wait(gate.at[i], 1)
+
+    def send_after_answer(in_x):
+        for i, (dx, dy) in enumerate(ORDER):
+            if (dx != 0) == in_x:
+                answered(i, later[i])
+                for kind in range(4):
+                    send(kind, i, later[i])
 
     def sent(kind):
         for i, (dx, dy) in dirs(kind):
@@ -145,8 +159,44 @@
             def _(i=i, dx=dx, dy=dy):
                 message(kind, i, dx, dy).wait_recv()
 
-    for kind_id in range(4):
-        send(kind_id)
+    for kind in (0, 1):
+        for i in range(len(ORDER)):
+            send(kind, i, earlier[i])
+    for i, ((_, _, device), cond) in enumerate(zip(mates, earlier)):
+        other = ORDER.index(tuple(-d for d in ORDER[i])) if i < len(ORDER) else 2 * len(ORDER) + n_ev - 2 - i
+
+        @pl.when(cond)
+        def _(device=device, other=other):
+            pl.semaphore_signal(gate.at[other], inc=1, device_id=device, device_id_type=MESH)
+    for kind in (2, 3):
+        for i in range(len(ORDER)):
+            send(kind, i, earlier[i])
+    for c in local:
+        c.start()
+
+    for d in (-1, 1):
+        lo = B + B // 2 if d < 0 else B
+        cl = 3 if d < 0 else 2
+        x_fill, y_fill = pl.ds(lo, B // 2), pl.ds(lo, B // 2)
+
+        @pl.when(jnp.logical_not(has_x[d]))
+        def _(x_fill=x_fill, cl=cl, lo=lo, d=d):
+            A[:, x_fill] = jnp.zeros((3, B // 2, EXT, depth), F32)
+            V[:, x_fill] = jnp.zeros((3, B // 2, EXT, depth), F32)
+            fx = EXT - 1 if d < 0 else B
+            for t in range(1, steps + 1):
+                F[t, :, fx] = jnp.zeros((3, EXT, depth), F32)
+            C[:, cl] = jnp.zeros((3, 4, C.shape[3]), F32)
+
+        @pl.when(jnp.logical_not(has_y[d]))
+        def _(y_fill=y_fill, cl=cl):
+            A[:, :, y_fill] = jnp.zeros((3, EXT, B // 2, depth), F32)
+            V[:, :, y_fill] = jnp.zeros((3, EXT, B // 2, depth), F32)
+            for t in range(1, steps + 1):
+                F[t, :, :, y_fill] = jnp.zeros((3, EXT, B // 2, depth), F32)
+            C[:, :, pl.ds(cl, 1)] = jnp.zeros((3, 4, 1, C.shape[3]), F32)
+
+    send_after_answer(False)
 
     local[4].wait()
     local[5].wait()
@@ -174,6 +224,8 @@
                 b = jnp.where(at_z, piece, 0.0).astype(BF16)
                 spread = spread + lax.dot_general(OH[...], b, (((1,), (1,)), ((), ())), preferred_element_type=F32)
             Q[3 * n + c] = spread.reshape(EXT, EXT, depth)
+
+    send_after_answer(True)
 
     nzc = C.shape[3]
     zi = lax.broadcasted_iota(jnp.int32, (nzc, depth), 0)
@@ -352,7 +404,8 @@
     parts = [pltpu.make_async_remote_copy(
         src_ref=T, dst_ref=G.at[o], send_sem=gssem.at[o], recv_sem=grsem.at[o],
         device_id={"event": lax.rem(ev + o, n_ev)}, device_id_type=MESH) for o in range(1, n_ev)]
-    for c in parts:
+    for o, c in enumerate(parts):
+        answered(len(ORDER) + o, later[len(ORDER) + o])
         c.start()
 
     def finish(x):
@@ -436,6 +489,7 @@
                 pltpu.SemaphoreType.DMA((4, 8)),
                 pltpu.SemaphoreType.DMA((n_ev,)),
                 pltpu.SemaphoreType.DMA((n_ev,)),
+                pltpu.SemaphoreType.REGULAR((len(DIRS) + n_ev - 1,)),
             ],
             compiler_params=pltpu.CompilerParams(collective_id=0, has_side_effects=True),
         )(adjoint, velocity, forward, receivers, jnp.swapaxes(residual, 1, 2), params)

time: 35.5 us -> 34.1 us (0.961)
  Pallas kernels: 34.7 us -> 33.3 us
    pallas_call x1, Pallas kernels: 34 us -> 32.6 us  [on_device(): pl.pallas_call(functools.partial(kernel, sizes), out_shape=(pltpu.VMEM(ad...]
where the time goes in v4:
time: 34.1 us; the launch traced here: 33.9 us
  Pallas kernels  33.3 us (98%)
  between operations  0.64 us (2%)
    pallas_call x1, Pallas kernels, on_device(): pl.pallas_call(functools.partial(kernel, sizes), out_shape=(pltpu.VMEM(ad...  32.6 us

profile of v4, /device:TPU:63, one launch (start us, length us, event | category | flops | bytes accessed | tf_op | source)
XLA Modules:
  0.0 33.9 jit_solution(9804230712856245349)
XLA Ops:
  0.6 32.6 %shard_map.77 = (f32[1,3,8,8,128]{4,3,2,1,0:T(8,128)S(1)}, f32[3,2,2,4]{3,2,1,0:T(2,128)S(1)}) custom-call(f32[1,3,8,8,128]{4,3,2,1,0:T(8,128)} %adj.1, f32[1,3,8,8,128]{4,3,2,1,0:T(8,128)} %vel.1, f32[1,4,3,8,8,128]{5,4,3,2,1,0:T(8,128)} %fwd.1, s32[1,512]{1,0:T(1,128)} %rec.1, f32[1,3,2,512]{3,2,1,0:T(2,128)} %bitcast.1, f32[3,2,2,32]{3,2,1,0:T(2,128)} %par.1), custom_call_target="tpu_custom_call" | custom-call | tf_op jit(solution)/shard_map/pallas_call | solution.py:457
  33.2 0.7 %shard_map.78 = (f32[1,3,8,8,128]{4,3,2,1,0:T(8,128)}, f32[3,2,2,4]{3,2,1,0:T(2,128)}) custom-call(f32[1,3,8,8,128]{4,3,2,1,0:T(8,128)S(1)} %get-tuple-element.4.aend, f32[3,2,2,4]{3,2,1,0:T(2,128)S(1)} %get-tuple-element.5.grad), custom_call_target="tpu_custom_call" | custom-call | tf_op jit(solution)/shard_map/pallas_call | solution.py:496

commit v5 on v4

--- a/solution.py
+++ b/solution.py
@@ -17,6 +17,7 @@
 UNROLL = 4
 DIRS = [(dx, dy) for dx in (-1, 0, 1) for dy in (-1, 0, 1) if (dx, dy) != (0, 0)]
 ORDER = sorted(DIRS, key=lambda d: (d[0] == 0, d[0] != 0 and d[1] != 0))
+FACES = [i for i, d in enumerate(ORDER) if 0 in d]
 
 
 def span(d, w, own):
@@ -41,7 +42,7 @@
 
 def kernel(sizes, adj, vel, fwd, rec, res, par, aend, grad,
            A, A1, V, F, C, C2, ZF, PF, REC, RES, OH, Q, S0, S1, E0, E1, FS, AC, KX, T, G,
-           lsem, ssem, rsem, gssem, grsem, gate):
+           lsem, ssem, rsem, rsem_faces, gsem, gate):
     n_gx, n_gy, n_ev, depth, ratio, steps = sizes
     gx, gy, ev = lax.axis_index("gx"), lax.axis_index("gy"), lax.axis_index("event")
     has_x = {-1: gx > 0, 1: gx < n_gx - 1}
@@ -56,25 +57,33 @@
 
     n_z, n_x = n_gx // 2, n_ev
 
-    def turn(px, py, pe):
-        z, y = lax.rem(px, n_z), py
-        x, core = (px // n_z) * (n_ev // 2) + pe // 2, lax.rem(pe, 2)
-
-        def hops(v, n):
-            return v + (2 * v > n).astype(jnp.int32) * (n - 2 * v)
-        place = ((z * n_gy + y) * n_x + x) * 2 + core
-        root = (place == 0).astype(jnp.int32)
-        late = 13 * place - 400 * core + 800 * (hops(z, n_z) + hops(y, n_gy) + hops(x, n_x)) + root * 20000
-        return late * 2048 + place
-
-    my_turn = turn(gx, gy, ev)
+    def late(v, n, step):
+        return 13 * step * v + 800 * (v + (2 * v > n).astype(jnp.int32) * (n - 2 * v)), step * v
+
+    def add(*terms):
+        return sum(t[0] for t in terms), sum(t[1] for t in terms)
+
+    def of_gx(px, pe):
+        return add(late(lax.rem(px, n_z), n_z, 2 * n_x * n_gy), late((px // n_z) * (n_ev // 2) + pe // 2, n_x, 2))
+
+    def of_core(pe):
+        core = lax.rem(pe, 2)
+        return -387 * core, core
+
+    def turn(*terms):
+        when, place = add(*terms)
+        return (when + (place == 0).astype(jnp.int32) * 20000) * 2048 + place
+
+    in_gx = {d: of_gx(gx + d, ev) for d in (-1, 0, 1)}
+    in_gy = {d: late(gy + d, n_gy, 2 * n_x) for d in (-1, 0, 1)}
+    core = of_core(ev)
+    my_turn = turn(in_gx[0], in_gy[0], core)
     mates = []
     for dx, dy in ORDER:
-        exists = there(dx, dy)
-        mates.append((exists, turn(gx + dx, gy + dy, ev) > my_turn, {"gx": gx + dx, "gy": gy + dy}))
+        mates.append((there(dx, dy), turn(in_gx[dx], in_gy[dy], core) > my_turn, {"gx": gx + dx, "gy": gy + dy}))
     for o in range(1, n_ev):
         mate = lax.rem(ev + o, n_ev)
-        mates.append((None, turn(gx, gy, mate) > my_turn, {"event": mate}))
+        mates.append((None, turn(of_gx(gx, mate), in_gy[0], of_core(mate)) > my_turn, {"event": mate}))
     later, earlier = [], []
     for exists, after, _ in mates:
         later.append(after if exists is None else jnp.logical_and(exists, after))
@@ -96,81 +105,103 @@
     local = [
         pltpu.make_async_copy(adj.at[0], A.at[:, own, own, :], lsem.at[0]),
         pltpu.make_async_copy(par, C.at[:, pl.ds(0, 2), pl.ds(0, 2), :], lsem.at[1]),
-        pltpu.make_async_copy(vel.at[0], V.at[:, own, own, :], lsem.at[2]),
-        pltpu.make_async_copy(fwd.at[0], F.at[:, :, own, own, :], lsem.at[3]),
-        pltpu.make_async_copy(rec, REC, lsem.at[4]),
-        pltpu.make_async_copy(res.at[0], RES, lsem.at[5]),
+        pltpu.make_async_copy(vel.at[0], V.at[:, own, own, :], lsem.at[0]),
+        pltpu.make_async_copy(fwd.at[0], F.at[:, :, own, own, :], lsem.at[0]),
+        pltpu.make_async_copy(rec, REC, lsem.at[2]),
+        pltpu.make_async_copy(res.at[0], RES, lsem.at[3]),
     ]
-    def message(kind, i, dx, dy):
+
+    def bytes_of(ref, sem):
+        return pltpu.make_async_copy(ref, ref, sem)
+
+    def messages(kind, i):
+        dx, dy = ORDER[i]
         corner = dx != 0 and dy != 0
+        pairs = []
+
+        def layer(src, dst, wx, wy, size, at=0):
+            (sx, tx), (sy, ty) = span(dx, wx, size), span(dy, wy, size)
+            if at:
+                sx = pl.ds(size - at if dx > 0 else at - 1, 1)
+                tx = pl.ds(2 * size - at if dx > 0 else size + at - 1, 1)
+            pairs.append((src(sx, sy), dst(tx, ty)))
+
         if kind == 0:
-            (sx, tx), (sy, ty) = span(dx, 1, 2), span(dy, 1, 2)
-            src, dst = par.at[:, sx, sy, :], C.at[:, tx, ty, :]
+            layer(lambda x, y: par.at[:, x, y, :], lambda x, y: C.at[:, x, y, :], 1, 1, 2)
+        elif kind == 1 and corner:
+            for at in (1, 2, 3):
+                layer(lambda x, y: adj.at[0, :, x, y, :], lambda x, y: A.at[:, x, y, :], 1, 4 - at, B, at)
+            layer(lambda x, y: vel.at[0, :, x, y, :], lambda x, y: V.at[:, x, y, :], 1, 1, B)
         elif kind == 1:
-            w = 3 if corner else 4
-            (sx, tx), (sy, ty) = span(dx, w, B), span(dy, w, B)
-            src, dst = adj.at[0, :, sx, sy, :], A.at[:, tx, ty, :]
-        elif kind == 2:
-            w = 1 if corner else 2
-            (sx, tx), (sy, ty) = span(dx, w, B), span(dy, w, B)
-            src, dst = vel.at[0, :, sx, sy, :], V.at[:, tx, ty, :]
-        else:
-            (sx, tx), (sy, ty) = span(dx, 1, B), span(dy, 1, B)
-            lv = pl.ds(1, steps)
-            src, dst = fwd.at[0, lv, :, sx, sy, :], F.at[lv, :, tx, ty, :]
-        return pltpu.make_async_remote_copy(
-            src_ref=src, dst_ref=dst, send_sem=ssem.at[kind, i], recv_sem=rsem.at[kind, i],
-            device_id={"gx": gx + dx, "gy": gy + dy}, device_id_type=MESH)
-
-    def dirs(kind):
-        return [(i, d) for i, d in enumerate(ORDER) if kind != 3 or 0 in d]
+            layer(lambda x, y: adj.at[0, :, x, y, :], lambda x, y: A.at[:, x, y, :], 4, 4, B)
+        elif not corner:
+            levels = pl.ds(1, steps)
+            layer(lambda x, y: vel.at[0, :, x, y, :], lambda x, y: V.at[:, x, y, :], 2, 2, B)
+            layer(lambda x, y: fwd.at[0, levels, :, x, y, :], lambda x, y: F.at[levels, :, x, y, :], 1, 1, B)
+        send_sem = ssem.at[0 if kind == 0 else 1, i]
+        recv_sem = rsem_faces.at[FACES.index(i)] if kind == 2 else rsem.at[min(kind, 1), i]
+        return [pltpu.make_async_remote_copy(
+            src_ref=src, dst_ref=dst, send_sem=send_sem, recv_sem=recv_sem,
+            device_id={"gx": gx + dx, "gy": gy + dy}, device_id_type=MESH) for src, dst in pairs]
+
+    def wait_rows(n, sem):
+        bytes_of(A1.at[:, pl.ds(0, n // B), pl.ds(0, B)] if n % B == 0 else A1.at[:, pl.ds(0, 1), pl.ds(0, n)], sem).wait()
 
     def send(kind, i, cond):
-        dx, dy = ORDER[i]
-        if kind != 3 or 0 in (dx, dy):
-            @pl.when(cond)
-            def _():
-                message(kind, i, dx, dy).start()
-
-    def answered(i, cond):
         @pl.when(cond)
         def _():
-            pl.semaphore_wait(gate.at[i], 1)
-
-    def send_after_answer(in_x):
+            for m in messages(kind, i):
+                m.start()
+
+    def sent():
+        for i, d in enumerate(ORDER):
+            @pl.when(there(*d))
+            def _(i=i, d=d):
+                messages(0, i)[0].wait_send()
+                wait_rows(7 if 0 not in d else (6 + steps) * B, ssem.at[1, i])
+
+    def arrived(kind, from_x):
         for i, (dx, dy) in enumerate(ORDER):
-            if (dx != 0) == in_x:
-                answered(i, later[i])
-                for kind in range(4):
+            corner = dx != 0 and dy != 0
+            if (dx != 0) != from_x or (kind == 2 and corner):
+                continue
+
+            @pl.when(there(-dx, -dy))
+            def _(i=i, corner=corner):
+                if kind == 0:
+                    messages(0, i)[0].wait_recv()
+                elif kind == 1:
+                    wait_rows(7 if corner else 4 * B, rsem.at[1, i])
+                else:
+                    wait_rows((2 + steps) * B, rsem_faces.at[FACES.index(i)])
+
+    def group(i):
+        return 2 if i >= len(ORDER) else int(ORDER[i][0] != 0)
+
+    def answered(which):
+        n = sum(c.astype(jnp.int32) for i, c in enumerate(later) if group(i) == which)
+
+        @pl.when(n > 0)
+        def _():
+            pl.semaphore_wait(gate.at[which], n)
+
+    def send_after_answer(which):
+        answered(which)
+        for kind in range(3):
+            for i in range(len(ORDER)):
+                if group(i) == which and (kind < 2 or 0 in ORDER[i]):
                     send(kind, i, later[i])
-
-    def sent(kind):
-        for i, (dx, dy) in dirs(kind):
-            @pl.when(there(dx, dy))
-            def _(i=i, dx=dx, dy=dy):
-                message(kind, i, dx, dy).wait_send()
-
-    def arrived(kind, from_x):
-        for i, (dx, dy) in dirs(kind):
-            if (dx != 0) != from_x:
-                continue
-
-            @pl.when(there(-dx, -dy))
-            def _(i=i, dx=dx, dy=dy):
-                message(kind, i, dx, dy).wait_recv()
 
     for kind in (0, 1):
         for i in range(len(ORDER)):
             send(kind, i, earlier[i])
     for i, ((_, _, device), cond) in enumerate(zip(mates, earlier)):
-        other = ORDER.index(tuple(-d for d in ORDER[i])) if i < len(ORDER) else 2 * len(ORDER) + n_ev - 2 - i
-
         @pl.when(cond)
-        def _(device=device, other=other):
-            pl.semaphore_signal(gate.at[other], inc=1, device_id=device, device_id_type=MESH)
-    for kind in (2, 3):
-        for i in range(len(ORDER)):
-            send(kind, i, earlier[i])
+        def _(device=device, which=group(i)):
+            pl.semaphore_signal(gate.at[which], inc=1, device_id=device, device_id_type=MESH)
+    for i in range(len(ORDER)):
+        if 0 in ORDER[i]:
+            send(2, i, earlier[i])
     for c in local:
         c.start()
 
@@ -196,7 +227,7 @@
                 F[t, :, :, y_fill] = jnp.zeros((3, EXT, B // 2, depth), F32)
             C[:, :, pl.ds(cl, 1)] = jnp.zeros((3, 4, 1, C.shape[3]), F32)
 
-    send_after_answer(False)
+    send_after_answer(0)
 
     local[4].wait()
     local[5].wait()
@@ -225,7 +256,7 @@
                 spread = spread + lax.dot_general(OH[...], b, (((1,), (1,)), ((), ())), preferred_element_type=F32)
             Q[3 * n + c] = spread.reshape(EXT, EXT, depth)
 
-    send_after_answer(True)
+    send_after_answer(1)
 
     nzc = C.shape[3]
     zi = lax.broadcasted_iota(jnp.int32, (nzc, depth), 0)
@@ -357,17 +388,16 @@
                 KX[m, x] = v if n == 0 else KX[m, x] + v
         return body
 
-    for c in local[:4]:
-        c.wait()
+    local[1].wait()
+    bytes_of(S0.at[:, pl.ds(0, 3 * EXT // 4)], lsem.at[0]).wait()
     inner(0, B, acceleration)
-    for kind_id in range(2):
-        arrived(kind_id, False)
+    arrived(0, False)
+    arrived(1, False)
     constants(0)
     inner(1, B - 1, stress(A, S0, E0))
     arrived(2, False)
     inner(2, B - 2, advance)
     inner(3, B - 3, stress(A1, S1, E1))
-    arrived(3, False)
     inner(1, B - 1, forward_strain)
     inner(1, B - 1, kernel_sums(A, E0, 0))
     inner(3, B - 3, kernel_sums(A1, E1, 1))
@@ -379,7 +409,6 @@
     arrived(2, True)
     outer(2, B - 2, 2, advance)
     outer(3, B - 3, 1, stress(A1, S1, E1))
-    arrived(3, True)
     outer(1, B - 1, 0, forward_strain)
     outer(1, B - 1, 0, kernel_sums(A, E0, 0))
     outer(3, B - 3, 0, kernel_sums(A1, E1, 1))
@@ -402,10 +431,10 @@
     wj = lax.broadcasted_iota(jnp.int32, (2 * depth, depth), 1)
     T[...] = times_ones(wide, jnp.where(wi // ratio == wj, 1.0, 0.0))
     parts = [pltpu.make_async_remote_copy(
-        src_ref=T, dst_ref=G.at[o], send_sem=gssem.at[o], recv_sem=grsem.at[o],
+        src_ref=T, dst_ref=G.at[o - 1], send_sem=gsem.at[0], recv_sem=gsem.at[1],
         device_id={"event": lax.rem(ev + o, n_ev)}, device_id_type=MESH) for o in range(1, n_ev)]
-    for o, c in enumerate(parts):
-        answered(len(ORDER) + o, later[len(ORDER) + o])
+    answered(2)
+    for c in parts:
         c.start()
 
     def finish(x):
@@ -414,15 +443,12 @@
         for c in range(3):
             aend[0, c, x] = 2.0 * A1[c, x, 0:B] - A[c, x, 0:B] + push * (f[c] + Q[3 + c, x, 0:B])
     inner(0, B, finish)
-    for kind_id in range(4):
-        sent(kind_id)
-    for c in parts:
-        c.wait_send()
-
+    sent()
+    bytes_of(G, gsem.at[0]).wait()
+    bytes_of(G, gsem.at[1]).wait()
     total = T[...]
-    for o, c in enumerate(parts):
-        c.wait_recv()
-        total = total + G[o + 1]
+    for o in range(n_ev - 1):
+        total = total + G[o]
     width = nzc // n_ev
     mine = pltpu.roll(total, lax.rem(depth - width * ev, depth), 1)
     other = pltpu.roll(mine, depth - nzc, 1)
@@ -483,13 +509,13 @@
                 vm((steps, 3, B, B, depth), F32),
                 vm((3, B, B, depth), F32),
                 vm((8, depth), F32),
-                vm((n_ev, 8, depth), F32),
-                pltpu.SemaphoreType.DMA((6,)),
-                pltpu.SemaphoreType.DMA((4, 8)),
-                pltpu.SemaphoreType.DMA((4, 8)),
-                pltpu.SemaphoreType.DMA((n_ev,)),
-                pltpu.SemaphoreType.DMA((n_ev,)),
-                pltpu.SemaphoreType.REGULAR((len(DIRS) + n_ev - 1,)),
+                vm((n_ev - 1, 8, depth), F32),
+                pltpu.SemaphoreType.DMA((4,)),
+                pltpu.SemaphoreType.DMA((2, len(ORDER))),
+                pltpu.SemaphoreType.DMA((2, len(ORDER))),
+                pltpu.SemaphoreType.DMA((len(FACES),)),
+                pltpu.SemaphoreType.DMA((2,)),
+                pltpu.SemaphoreType.REGULAR((3,)),
             ],
             compiler_params=pltpu.CompilerParams(collective_id=0, has_side_effects=True),
         )(adjoint, velocity, forward, receivers, jnp.swapaxes(residual, 1, 2), params)

time: 34.1 us -> 32.9 us (0.965)
  Pallas kernels: 33.3 us -> 32.1 us
    pallas_call x1, Pallas kernels: 32.6 us -> 31.4 us  [on_device(): pl.pallas_call(functools.partial(kernel, sizes), out_shape=(pltpu.VMEM(ad...]
where the time goes in v5:
time: 32.9 us; the launch traced here: 32.7 us
  Pallas kernels  32.1 us (98%)
  between operations  0.64 us (2%)
    pallas_call x1, Pallas kernels, on_device(): pl.pallas_call(functools.partial(kernel, sizes), out_shape=(pltpu.VMEM(ad...  31.4 us
    pallas_call x1, Pallas kernels, on_device(): pl.pallas_call(put_out, out_shape=tuple((jax.ShapeDtypeStruct(h.shape, F3...  0.66 us

profile of v5, /device:TPU:63, one launch (start us, length us, event | category | flops | bytes accessed | tf_op | source)
XLA Modules:
  0.0 32.7 jit_solution(1084848382980825966)
XLA Ops:
  0.6 31.4 %shard_map.77 = (f32[1,3,8,8,128]{4,3,2,1,0:T(8,128)S(1)}, f32[3,2,2,4]{3,2,1,0:T(2,128)S(1)}) custom-call(f32[1,3,8,8,128]{4,3,2,1,0:T(8,128)} %adj.1, f32[1,3,8,8,128]{4,3,2,1,0:T(8,128)} %vel.1, f32[1,4,3,8,8,128]{5,4,3,2,1,0:T(8,128)} %fwd.1, s32[1,512]{1,0:T(1,128)} %rec.1, f32[1,3,2,512]{3,2,1,0:T(2,128)} %bitcast.1, f32[3,2,2,32]{3,2,1,0:T(2,128)} %par.1), custom_call_target="tpu_custom_call" | custom-call | tf_op jit(solution)/shard_map/pallas_call | solution.py:483
  32.0 0.7 %shard_map.78 = (f32[1,3,8,8,128]{4,3,2,1,0:T(8,128)}, f32[3,2,2,4]{3,2,1,0:T(2,128)}) custom-call(f32[1,3,8,8,128]{4,3,2,1,0:T(8,128)S(1)} %get-tuple-element.4.aend, f32[3,2,2,4]{3,2,1,0:T(2,128)S(1)} %get-tuple-element.5.grad), custom_call_target="tpu_custom_call" | custom-call | tf_op jit(solution)/shard_map/pallas_call | solution.py:522

commit v6 on v5

--- a/solution.py
+++ b/solution.py
@@ -16,7 +16,7 @@
 EXT = 2 * B
 UNROLL = 4
 DIRS = [(dx, dy) for dx in (-1, 0, 1) for dy in (-1, 0, 1) if (dx, dy) != (0, 0)]
-ORDER = sorted(DIRS, key=lambda d: (d[0] == 0, d[0] != 0 and d[1] != 0))
+ORDER = sorted(DIRS, key=lambda d: (d[0] == 0, 0 in d))
 FACES = [i for i, d in enumerate(ORDER) if 0 in d]
 
 

time: 32.9 us -> 31.2 us (0.948)
  Pallas kernels: 32.1 us -> 30.4 us
    pallas_call x1, Pallas kernels: 31.4 us -> 29.7 us  [on_device(): pl.pallas_call(functools.partial(kernel, sizes), out_shape=(pltpu.VMEM(ad...]
where the time goes in v6:
time: 31.2 us; the launch traced here: 31 us
  Pallas kernels  30.4 us (97%)
  between operations  0.64 us (2%)
    pallas_call x1, Pallas kernels, on_device(): pl.pallas_call(functools.partial(kernel, sizes), out_shape=(pltpu.VMEM(ad...  29.7 us
    pallas_call x1, Pallas kernels, on_device(): pl.pallas_call(put_out, out_shape=tuple((jax.ShapeDtypeStruct(h.shape, F3...  0.66 us

profile of v6, /device:TPU:63, one launch (start us, length us, event | category | flops | bytes accessed | tf_op | source)
XLA Modules:
  0.0 31.0 jit_solution(14641397839113904551)
XLA Ops:
  0.6 29.7 %shard_map.77 = (f32[1,3,8,8,128]{4,3,2,1,0:T(8,128)S(1)}, f32[3,2,2,4]{3,2,1,0:T(2,128)S(1)}) custom-call(f32[1,3,8,8,128]{4,3,2,1,0:T(8,128)} %adj.1, f32[1,3,8,8,128]{4,3,2,1,0:T(8,128)} %vel.1, f32[1,4,3,8,8,128]{5,4,3,2,1,0:T(8,128)} %fwd.1, s32[1,512]{1,0:T(1,128)} %rec.1, f32[1,3,2,512]{3,2,1,0:T(2,128)} %bitcast.1, f32[3,2,2,32]{3,2,1,0:T(2,128)} %par.1), custom_call_target="tpu_custom_call" | custom-call | tf_op jit(solution)/shard_map/pallas_call | solution.py:483
  30.4 0.7 %shard_map.78 = (f32[1,3,8,8,128]{4,3,2,1,0:T(8,128)}, f32[3,2,2,4]{3,2,1,0:T(2,128)}) custom-call(f32[1,3,8,8,128]{4,3,2,1,0:T(8,128)S(1)} %get-tuple-element.4.aend, f32[3,2,2,4]{3,2,1,0:T(2,128)S(1)} %get-tuple-element.5.grad), custom_call_target="tpu_custom_call" | custom-call | tf_op jit(solution)/shard_map/pallas_call | solution.py:522

commit v7 on v6

--- a/solution.py
+++ b/solution.py
@@ -134,12 +134,13 @@
             layer(lambda x, y: vel.at[0, :, x, y, :], lambda x, y: V.at[:, x, y, :], 1, 1, B)
         elif kind == 1:
             layer(lambda x, y: adj.at[0, :, x, y, :], lambda x, y: A.at[:, x, y, :], 4, 4, B)
-        elif not corner:
+        elif kind == 2:
+            layer(lambda x, y: vel.at[0, :, x, y, :], lambda x, y: V.at[:, x, y, :], 2, 2, B)
+        else:
             levels = pl.ds(1, steps)
-            layer(lambda x, y: vel.at[0, :, x, y, :], lambda x, y: V.at[:, x, y, :], 2, 2, B)
             layer(lambda x, y: fwd.at[0, levels, :, x, y, :], lambda x, y: F.at[levels, :, x, y, :], 1, 1, B)
         send_sem = ssem.at[0 if kind == 0 else 1, i]
-        recv_sem = rsem_faces.at[FACES.index(i)] if kind == 2 else rsem.at[min(kind, 1), i]
+        recv_sem = rsem_faces.at[kind - 2, FACES.index(i)] if kind >= 2 else rsem.at[kind, i]
         return [pltpu.make_async_remote_copy(
             src_ref=src, dst_ref=dst, send_sem=send_sem, recv_sem=recv_sem,
             device_id={"gx": gx + dx, "gy": gy + dy}, device_id_type=MESH) for src, dst in pairs]
@@ -163,7 +164,7 @@
     def arrived(kind, from_x):
         for i, (dx, dy) in enumerate(ORDER):
             corner = dx != 0 and dy != 0
-            if (dx != 0) != from_x or (kind == 2 and corner):
+            if (dx != 0) != from_x or (kind >= 2 and corner):
                 continue
 
             @pl.when(there(-dx, -dy))
@@ -173,10 +174,10 @@
                 elif kind == 1:
                     wait_rows(7 if corner else 4 * B, rsem.at[1, i])
                 else:
-                    wait_rows((2 + steps) * B, rsem_faces.at[FACES.index(i)])
+                    wait_rows((2 if kind == 2 else steps) * B, rsem_faces.at[kind - 2, FACES.index(i)])
 
     def group(i):
-        return 2 if i >= len(ORDER) else int(ORDER[i][0] != 0)
+        return 2 if i >= len(ORDER) else 3 if 0 not in ORDER[i] else int(ORDER[i][0] != 0)
 
     def answered(which):
         n = sum(c.astype(jnp.int32) for i, c in enumerate(later) if group(i) == which)
@@ -187,7 +188,7 @@
 
     def send_after_answer(which):
         answered(which)
-        for kind in range(3):
+        for kind in range(4):
             for i in range(len(ORDER)):
                 if group(i) == which and (kind < 2 or 0 in ORDER[i]):
                     send(kind, i, later[i])
@@ -199,9 +200,13 @@
         @pl.when(cond)
         def _(device=device, which=group(i)):
             pl.semaphore_signal(gate.at[which], inc=1, device_id=device, device_id_type=MESH)
-    for i in range(len(ORDER)):
-        if 0 in ORDER[i]:
-            send(2, i, earlier[i])
+    def send_rest(which):
+        for kind in (2, 3):
+            for i in FACES:
+                if group(i) == which:
+                    send(kind, i, earlier[i])
+
+    send_rest(0)
     for c in local:
         c.start()
 
@@ -226,8 +231,6 @@
             for t in range(1, steps + 1):
                 F[t, :, :, y_fill] = jnp.zeros((3, EXT, B // 2, depth), F32)
             C[:, :, pl.ds(cl, 1)] = jnp.zeros((3, 4, 1, C.shape[3]), F32)
-
-    send_after_answer(0)
 
     local[4].wait()
     local[5].wait()
@@ -256,6 +259,8 @@
                 spread = spread + lax.dot_general(OH[...], b, (((1,), (1,)), ((), ())), preferred_element_type=F32)
             Q[3 * n + c] = spread.reshape(EXT, EXT, depth)
 
+    send_rest(1)
+    send_after_answer(0)
     send_after_answer(1)
 
     nzc = C.shape[3]
@@ -398,9 +403,12 @@
     arrived(2, False)
     inner(2, B - 2, advance)
     inner(3, B - 3, stress(A1, S1, E1))
+    arrived(3, False)
     inner(1, B - 1, forward_strain)
     inner(1, B - 1, kernel_sums(A, E0, 0))
     inner(3, B - 3, kernel_sums(A1, E1, 1))
+
+    send_after_answer(3)
 
     arrived(0, True)
     constants(1)
@@ -409,6 +417,7 @@
     arrived(2, True)
     outer(2, B - 2, 2, advance)
     outer(3, B - 3, 1, stress(A1, S1, E1))
+    arrived(3, True)
     outer(1, B - 1, 0, forward_strain)
     outer(1, B - 1, 0, kernel_sums(A, E0, 0))
     outer(3, B - 3, 0, kernel_sums(A1, E1, 1))
@@ -513,9 +522,9 @@
                 pltpu.SemaphoreType.DMA((4,)),
                 pltpu.SemaphoreType.DMA((2, len(ORDER))),
                 pltpu.SemaphoreType.DMA((2, len(ORDER))),
-                pltpu.SemaphoreType.DMA((len(FACES),)),
+                pltpu.SemaphoreType.DMA((2, len(FACES))),
                 pltpu.SemaphoreType.DMA((2,)),
-                pltpu.SemaphoreType.REGULAR((3,)),
+                pltpu.SemaphoreType.REGULAR((4,)),
             ],
             compiler_params=pltpu.CompilerParams(collective_id=0, has_side_effects=True),
         )(adjoint, velocity, forward, receivers, jnp.swapaxes(residual, 1, 2), params)

time: 31.2 us -> 30.4 us (0.974)
  the two profiles are of different devices: /device:TPU:63 before, /device:TPU:111 now
where the time goes in v7:
time: 30.4 us; the launch traced here: 30.3 us
  Pallas kernels  29.6 us (97%)
  between operations  0.64 us (2%)
    pallas_call x1, Pallas kernels, on_device(): pl.pallas_call(functools.partial(kernel, sizes), out_shape=(pltpu.VMEM(ad...  29 us
    pallas_call x1, Pallas kernels, on_device(): pl.pallas_call(put_out, out_shape=tuple((jax.ShapeDtypeStruct(h.shape, F3...  0.66 us

profile of v7, /device:TPU:111, one launch (start us, length us, event | category | flops | bytes accessed | tf_op | source)
XLA Modules:
  0.0 30.3 jit_solution(3576229283294366074)
XLA Ops:
  0.6 29.0 %shard_map.77 = (f32[1,3,8,8,128]{4,3,2,1,0:T(8,128)S(1)}, f32[3,2,2,4]{3,2,1,0:T(2,128)S(1)}) custom-call(f32[1,3,8,8,128]{4,3,2,1,0:T(8,128)} %adj.1, f32[1,3,8,8,128]{4,3,2,1,0:T(8,128)} %vel.1, f32[1,4,3,8,8,128]{5,4,3,2,1,0:T(8,128)} %fwd.1, s32[1,512]{1,0:T(1,128)} %rec.1, f32[1,3,2,512]{3,2,1,0:T(2,128)} %bitcast.1, f32[3,2,2,32]{3,2,1,0:T(2,128)} %par.1), custom_call_target="tpu_custom_call" | custom-call | tf_op jit(solution)/shard_map/pallas_call | solution.py:492
  29.6 0.7 %shard_map.78 = (f32[1,3,8,8,128]{4,3,2,1,0:T(8,128)}, f32[3,2,2,4]{3,2,1,0:T(2,128)}) custom-call(f32[1,3,8,8,128]{4,3,2,1,0:T(8,128)S(1)} %get-tuple-element.4.aend, f32[3,2,2,4]{3,2,1,0:T(2,128)S(1)} %get-tuple-element.5.grad), custom_call_target="tpu_custom_call" | custom-call | tf_op jit(solution)/shard_map/pallas_call | solution.py:531

commit v8 on v7

--- a/solution.py
+++ b/solution.py
@@ -258,8 +258,9 @@
                 b = jnp.where(at_z, piece, 0.0).astype(BF16)
                 spread = spread + lax.dot_general(OH[...], b, (((1,), (1,)), ((), ())), preferred_element_type=F32)
             Q[3 * n + c] = spread.reshape(EXT, EXT, depth)
-
-    send_rest(1)
+        if n == 0:
+            send_rest(1)
+
     send_after_answer(0)
     send_after_answer(1)
 

time: 30.4 us -> 31.1 us (1.023)
  the two profiles are of different devices: /device:TPU:111 before, /device:TPU:31 now
where the time goes in v8:
time: 31.1 us; the launch traced here: 30.9 us
  Pallas kernels  30.3 us (97%)
  between operations  0.64 us (2%)
    pallas_call x1, Pallas kernels, on_device(): pl.pallas_call(functools.partial(kernel, sizes), out_shape=(pltpu.VMEM(ad...  29.6 us
    pallas_call x1, Pallas kernels, on_device(): pl.pallas_call(put_out, out_shape=tuple((jax.ShapeDtypeStruct(h.shape, F3...  0.66 us

profile of v8, /device:TPU:31, one launch (start us, length us, event | category | flops | bytes accessed | tf_op | source)
XLA Modules:
  0.0 30.9 jit_solution(17136234440840924515)
XLA Ops:
  0.6 29.6 %shard_map.77 = (f32[1,3,8,8,128]{4,3,2,1,0:T(8,128)S(1)}, f32[3,2,2,4]{3,2,1,0:T(2,128)S(1)}) custom-call(f32[1,3,8,8,128]{4,3,2,1,0:T(8,128)} %adj.1, f32[1,3,8,8,128]{4,3,2,1,0:T(8,128)} %vel.1, f32[1,4,3,8,8,128]{5,4,3,2,1,0:T(8,128)} %fwd.1, s32[1,512]{1,0:T(1,128)} %rec.1, f32[1,3,2,512]{3,2,1,0:T(2,128)} %bitcast.1, f32[3,2,2,32]{3,2,1,0:T(2,128)} %par.1), custom_call_target="tpu_custom_call" | custom-call | tf_op jit(solution)/shard_map/pallas_call | solution.py:493
  30.3 0.7 %shard_map.78 = (f32[1,3,8,8,128]{4,3,2,1,0:T(8,128)}, f32[3,2,2,4]{3,2,1,0:T(2,128)}) custom-call(f32[1,3,8,8,128]{4,3,2,1,0:T(8,128)S(1)} %get-tuple-element.4.aend, f32[3,2,2,4]{3,2,1,0:T(2,128)S(1)} %get-tuple-element.5.grad), custom_call_target="tpu_custom_call" | custom-call | tf_op jit(solution)/shard_map/pallas_call | solution.py:532
